TPU v7x, 32 devices: a whole 2x2x4 slice. The times are simulated.
32 devices in a mesh: stream: 2 (over core), batch: 16 (over z, y, x).
Axes of the slice: x: 2, y: 2, z: 4, core: 2. Of those that a mesh axis runs over, the one named last changes fastest.
Arguments:
- inputs: bfloat16 [2, 16, 1024, 768], P('stream', 'batch'), may hold values from -6 to 6
- lengths: int32 [16], P('batch'), may hold values from 128 to 1024, as said below
- cotangent: bfloat16 [2, 16, 1024, 768], P('stream', 'batch'), may hold values from -6 to 6
- qkv_weight: bfloat16 [768, 2304], replicated, may hold values from -0.21875 to 0.21875
- out_weight: bfloat16 [768, 768], replicated, may hold values from -2 to 2
- up_weight: bfloat16 [768, 3072], replicated, may hold values from -0.21875 to 0.21875
- down_weight: bfloat16 [3072, 768], replicated, may hold values from -0.109375 to 0.109375
- attn_gain: float32 [768], replicated, may hold values from 0.5 to 1.5
- mlp_gain: float32 [768], replicated, may hold values from 0.5 to 1.5
Outputs:
- outputs: bfloat16 [2, 16, 1024, 768], P('stream', 'batch')
- input_grad: bfloat16 [2, 16, 1024, 768], P('stream', 'batch')
- qkv_grad: float32 [768, 2304], P(('stream', 'batch'))
- out_grad: float32 [768, 768], P(('stream', 'batch'))
- up_grad: float32 [768, 3072], P(None, ('stream', 'batch'))
- down_grad: float32 [3072, 768], P(('stream', 'batch'))
- attn_gain_grad: float32 [768], replicated
- mlp_gain_grad: float32 [768], replicated
- rms: float32 [3], replicated
Inputs may be any that keep to these rules, and one draw needn't show every extreme that they name: `lengths`: each length is a multiple of 16; some row has length 1024.
All inputs are finite; a program needn't handle non-finite values.
Results may differ from a plain program's by a relative error of at most 0.014.
Values may be sent and summed in bfloat16 or wider, within the bound.
No kernel may reach another device: no remote copies, remote signals or barrier semaphores. Data moves between devices by JAX's collectives and lax.ppermute only.
A program may use at most 384 MiB of HBM per device.

v0:
```python
import jax
import jax.numpy as jnp
from jax import lax
from jax.sharding import PartitionSpec as P

H = 12
HD = 64
BLK = 16


EPS = 1e-06
NEG = -1e30


def shifted(array, axis, by):
    peers = lax.axis_size(axis)
    pairs = [(i, i + by) for i in range(peers) if 0 <= i + by < peers]
    return lax.ppermute(array, axis, pairs)


def shortened(array):
    return jax.tree.map(lambda a: a.astype(jnp.bfloat16) if a.dtype == jnp.float32 else a, array)


def rms_norm(value, gain):
    return value * lax.rsqrt(jnp.mean(value * value, axis=-1, keepdims=True) + EPS) * gain


def rotary_tables(length, width):
    half = width // 2
    freqs = jnp.exp(-jnp.log(10000.0) * jnp.arange(half, dtype=jnp.float32) / half)
    angles = jnp.arange(length, dtype=jnp.float32)[:, None] * freqs[None, :]
    return (jnp.cos(angles)[:, None, :], jnp.sin(angles)[:, None, :])


def rotate(tensor, cosine, sine, sign):
    half = tensor.shape[-1] // 2
    first = tensor[..., :half]
    second = tensor[..., half:]
    return jnp.concatenate(
        [first * cosine - sign * second * sine, second * cosine + sign * first * sine], axis=-1
    )


def on_device(
    inputs, lengths, cotangent, qkv_weight, out_weight, up_weight, down_weight, attn_gain, mlp_gain
):
    rows, seq, width = (inputs.shape[1], inputs.shape[2], inputs.shape[3])
    tokens = rows * seq
    qblock = min(seq, 512)
    scale = HD ** (-0.5)
    noisy = lax.axis_index("stream") == 1
    position = jnp.arange(seq, dtype=jnp.int32)
    block = position // BLK
    cosine, sine = rotary_tables(seq, HD)

    def key_mask(length, query_block):
        valid = (position < length)[None, :]
        own = jnp.where(
            noisy, block[None, :] == query_block[:, None], block[None, :] <= query_block[:, None]
        )
        other = jnp.logical_and(noisy, block[None, :] < query_block[:, None])
        return jnp.concatenate([own & valid, other & valid], axis=1)

    def scores_of(q_part, k_row, length, start):
        raw = jnp.einsum("qhd,khd->hqk", q_part, k_row, preferred_element_type=jnp.float32) * scale
        mask = key_mask(length, block[start : start + qblock])
        return jnp.where(mask[None], raw, NEG)

    x = inputs[0].astype(jnp.float32).reshape(tokens, width)
    h1 = rms_norm(x, attn_gain).astype(jnp.bfloat16)
    qkv = jnp.dot(h1, qkv_weight, preferred_element_type=jnp.float32).reshape(rows, seq, 3, H, HD)
    query = rotate(qkv[:, :, 0], cosine, sine, 1.0).astype(jnp.bfloat16)
    key = rotate(qkv[:, :, 1], cosine, sine, 1.0).astype(jnp.bfloat16).reshape(rows, seq, width)
    value = qkv[:, :, 2].astype(jnp.bfloat16).reshape(rows, seq, width)
    key_part, value_part = shifted((key, value), "stream", 1)
    keys = jnp.concatenate([key, key_part], axis=1).reshape(rows, 2 * seq, H, HD)
    values = jnp.concatenate([value, value_part], axis=1).reshape(rows, 2 * seq, H, HD)

    def forward_row(item):
        q_row, k_row, v_row, length = item
        outs, tops, totals = ([], [], [])
        for start in range(0, seq, qblock):
            scores = scores_of(q_row[start : start + qblock], k_row, length, start)
            top = jnp.max(scores, axis=-1, keepdims=True)
            expo = jnp.exp(scores - top)
            total = jnp.sum(expo, axis=-1, keepdims=True)
            prob = (expo / total).astype(jnp.bfloat16)
            outs.append(jnp.einsum("hqk,khd->qhd", prob, v_row, preferred_element_type=jnp.float32))
            tops.append(top)
            totals.append(total)
        return (jnp.concatenate(outs, 0), jnp.concatenate(tops, 1), jnp.concatenate(totals, 1))

    attended, tops, totals = lax.map(forward_row, (query, keys, values, lengths))
    attn_out = attended.reshape(tokens, width).astype(jnp.bfloat16)
    branch = jnp.dot(attn_out, out_weight, preferred_element_type=jnp.float32)
    x2 = x + branch
    h2 = rms_norm(x2, mlp_gain).astype(jnp.bfloat16)
    upper = jnp.dot(h2, up_weight, preferred_element_type=jnp.float32)
    gelu_of = lambda v: jax.nn.gelu(v, approximate=True)
    act = gelu_of(upper).astype(jnp.bfloat16)
    mixed = jnp.dot(act, down_weight, preferred_element_type=jnp.float32)
    outputs = (x2 + mixed).astype(jnp.bfloat16).reshape(1, rows, seq, width)
    weight = (position[None, :] < lengths[:, None]).astype(jnp.float32).reshape(tokens, 1)
    sums = jnp.stack(
        [
            jnp.sum(weight * x * x),
            jnp.sum(weight * branch * branch),
            jnp.sum(weight * mixed * mixed),
        ]
    )
    count = jnp.sum(lengths).astype(jnp.float32)
    totals_sq, counted = lax.psum((sums, count), ("stream", "batch"))
    grad_out = cotangent[0].astype(jnp.float32).reshape(tokens, width)
    grad_mixed = grad_out.astype(jnp.bfloat16)
    down_grad = jnp.einsum("tf,td->fd", act, grad_mixed, preferred_element_type=jnp.float32)
    grad_act = jnp.einsum("td,fd->tf", grad_mixed, down_weight, preferred_element_type=jnp.float32)
    gelu_pull = jax.vjp(gelu_of, upper)[1]
    grad_upper = gelu_pull(grad_act)[0].astype(jnp.bfloat16)
    up_grad = jnp.einsum("td,tf->df", h2, grad_upper, preferred_element_type=jnp.float32)
    grad_h2 = jnp.einsum("tf,df->td", grad_upper, up_weight, preferred_element_type=jnp.float32)
    norm_pull = jax.vjp(rms_norm, x2, mlp_gain)[1]
    grad_x2_norm, mlp_gain_grad = norm_pull(grad_h2)
    grad_x2 = grad_out + grad_x2_norm
    grad_branch = grad_x2.astype(jnp.bfloat16)
    out_grad = jnp.einsum("ti,tj->ij", attn_out, grad_branch, preferred_element_type=jnp.float32)
    grad_attn = jnp.einsum("tj,ij->ti", grad_branch, out_weight, preferred_element_type=jnp.float32)
    grad_attn = grad_attn.astype(jnp.bfloat16).reshape(rows, seq, H, HD)

    def backward_row(item):
        q_row, k_row, v_row, g_row, top_row, total_row, length = item
        grad_query = []
        grad_keys = jnp.zeros((2 * seq, H, HD), jnp.float32)
        grad_values = jnp.zeros((2 * seq, H, HD), jnp.float32)
        for start in range(0, seq, qblock):
            q_part = q_row[start : start + qblock]
            g_part = g_row[start : start + qblock]
            scores = scores_of(q_part, k_row, length, start)
            prob = (
                jnp.exp(scores - top_row[:, start : start + qblock])
                / total_row[:, start : start + qblock]
            )
            low_prob = prob.astype(jnp.bfloat16)
            grad_prob = jnp.einsum(
                "qhd,khd->hqk", g_part, v_row, preferred_element_type=jnp.float32
            )
            grad_scores = prob * (grad_prob - jnp.sum(prob * grad_prob, axis=-1, keepdims=True))
            grad_scores = grad_scores.astype(jnp.bfloat16)
            grad_query.append(
                jnp.einsum("hqk,khd->qhd", grad_scores, k_row, preferred_element_type=jnp.float32)
                * scale
            )
            grad_keys = (
                grad_keys
                + jnp.einsum(
                    "hqk,qhd->khd", grad_scores, q_part, preferred_element_type=jnp.float32
                )
                * scale
            )
            grad_values = grad_values + jnp.einsum(
                "hqk,qhd->khd", low_prob, g_part, preferred_element_type=jnp.float32
            )
        return (jnp.concatenate(grad_query, 0), grad_keys, grad_values)

    grad_q, grad_k_all, grad_v_all = lax.map(
        backward_row, (query, keys, values, grad_attn, tops, totals, lengths)
    )
    grad_k_all = grad_k_all.reshape(rows, 2 * seq, width)
    grad_v_all = grad_v_all.reshape(rows, 2 * seq, width)
    back_k, back_v = shifted(
        (shortened(grad_k_all[:, seq:]), shortened(grad_v_all[:, seq:])), "stream", -1
    )
    grad_k = (grad_k_all[:, :seq] + back_k).reshape(rows, seq, H, HD)
    grad_v = (grad_v_all[:, :seq] + back_v).reshape(rows, seq, H, HD)
    grad_q = rotate(grad_q, cosine, sine, -1.0)
    grad_k = rotate(grad_k, cosine, sine, -1.0)
    grad_qkv = (
        jnp.stack([grad_q, grad_k, grad_v], axis=2).reshape(tokens, 3 * width).astype(jnp.bfloat16)
    )
    qkv_grad = jnp.einsum("td,tc->dc", h1, grad_qkv, preferred_element_type=jnp.float32)
    grad_h1 = jnp.einsum("tc,dc->td", grad_qkv, qkv_weight, preferred_element_type=jnp.float32)
    first_pull = jax.vjp(rms_norm, x, attn_gain)[1]
    grad_x_norm, attn_gain_grad = first_pull(grad_h1)
    input_grad = (grad_x2 + grad_x_norm).astype(jnp.bfloat16).reshape(1, rows, seq, width)
    attn_gain_sum, mlp_gain_sum = lax.psum((attn_gain_grad, mlp_gain_grad), ("stream", "batch"))
    qkv_sum, out_sum, up_sum, down_sum = (
        lax.psum_scatter(qkv_grad, ("stream", "batch"), scatter_dimension=0, tiled=True),
        lax.psum_scatter(out_grad, ("stream", "batch"), scatter_dimension=0, tiled=True),
        lax.psum_scatter(up_grad, ("stream", "batch"), scatter_dimension=1, tiled=True),
        lax.psum_scatter(down_grad, ("stream", "batch"), scatter_dimension=0, tiled=True),
    )
    rms = jnp.sqrt(totals_sq / (counted * width))
    return (
        outputs,
        input_grad,
        qkv_sum,
        out_sum,
        up_sum,
        down_sum,
        attn_gain_sum,
        mlp_gain_sum,
        rms,
    )


def solution(mesh):
    return jax.shard_map(
        on_device,
        mesh=mesh,
        in_specs=(
            P("stream", "batch", None, None),
            P("batch"),
            P("stream", "batch", None, None),
            P(),
            P(),
            P(),
            P(),
            P(),
            P(),
        ),
        out_specs=(
            P("stream", "batch", None, None),
            P("stream", "batch", None, None),
            P(("stream", "batch"), None),
            P(("stream", "batch"), None),
            P(None, ("stream", "batch")),
            P(("stream", "batch"), None),
            P(),
            P(),
            P(),
        ),
        check_vma=False,
    )
```

profile of v0, /device:TPU:0, one launch (start us, length us, event | category | flops | bytes accessed | tf_op | source)
XLA Modules:
  0.0 892.0 jit_solution(158825215571995424)
XLA Ops:
  11.4 5.8 copy.32
  17.2 6.2 convolution_bitcast_fusion
  28.3 3.5 collective-permute-start.1
  46.1 3.6 slice_bitcast_fusion.2
  49.7 24.0 %fusion.122 = (f32[12,512]{1,0:T(8,128)}, f32[12,512,2048]{2,1,0:T(8,128)}) fusion(pred[512,2048]{1,0:T(8,128)(4,1)} %pad_add_fusion, bf16[1,1024,12,32]{1,3,2,0:T(8,128)(2,1)S(1)} %get-tuple-element.123, bf16[1,1024,12,32]{1,3,2,0:T(8,128)(2,1)} %get-tuple-element.124, bf16[1024,12,64]{0,2,1:T(8,128)(2,1)} %bitcast.16, bf16[1024,12,64]{0,2,1:T(8,128)(2,1)S(1)} %fusion.127), kind=kOutput, calls=%fused_computation.169 | convolution fusion | flops 1668810752 | bytes 56123392 | tf_op jit(solution)/shard_map/while/body/eval_jaxpr/sub | solution.py:86
  73.7 23.9 %fusion.117 = (f32[12,512]{1,0:T(8,128)}, f32[12,512,2048]{2,1,0:T(8,128)}) fusion(pred[512,2048]{1,0:T(8,128)(4,1)} %pad_add_fusion.1, bf16[1,1024,12,32]{1,3,2,0:T(8,128)(2,1)} %get-tuple-element.124, bf16[1,1024,12,32]{1,3,2,0:T(8,128)(2,1)S(1)} %get-tuple-element.123, bf16[1024,12,64]{0,2,1:T(8,128)(2,1)} %bitcast.16, ...), kind=kOutput, calls=%fused_computation.168 | convolution fusion | flops 1668810752 | bytes 56123392 | tf_op jit(solution)/shard_map/while/body/eval_jaxpr/sub | solution.py:86
  97.6 19.4 %fusion.74 = bf16[512,12,64]{0,2,1:T(8,128)(2,1)S(1)} fusion(bf16[1024,12,64]{0,2,1:T(8,128)(2,1)} %bitcast.9, bf16[1024,12,64]{0,2,1:T(8,128)(2,1)} %slice_bitcast_fusion.2, f32[12,512,2048]{2,1,0:T(8,128)} %get-tuple-element.143, f32[12,512]{1,0:T(8,128)} %get-tuple-element.142), kind=kOutput, calls=%fused_computation.125 | convolution fusion | flops 1642463232 | bytes 54288384 | tf_op jit(solution)/shard_map/while/body/eval_jaxpr/hqk,khd->qhd/dot_general | solution.py:89
  117.1 19.3 %fusion.77 = bf16[512,12,64]{0,2,1:T(8,128)(2,1)} fusion(bf16[1024,12,64]{0,2,1:T(8,128)(2,1)} %bitcast.9, bf16[1024,12,64]{0,2,1:T(8,128)(2,1)S(1)} %copy-done.25, f32[12,512,2048]{2,1,0:T(8,128)} %get-tuple-element.145, f32[12,512]{1,0:T(8,128)S(1)} %copy-done.42), kind=kOutput, calls=%fused_computation.126 | convolution fusion | flops 1642463232 | bytes 54288384 | tf_op jit(solution)/shard_map/while/body/eval_jaxpr/hqk,khd->qhd/dot_general | solution.py:89
  138.1 3.4 multiply_reduce_fusion.4
  141.5 5.3 fusion.101
  146.9 18.5 %fusion.16 = bf16[1024,3072]{1,0:T(8,128)(2,1)} fusion(f32[1024,3072]{1,0:T(8,128)S(1)} %fusion.101, bf16[3072,768]{1,0:T(8,128)(2,1)} %param.15, bf16[1,1,1024,768]{3,2,1,0:T(8,128)(2,1)} %param.11), kind=kOutput, calls=%fused_computation.28 | convolution fusion | flops 4894752768 | bytes 25165824 | tf_op jit(solution)/shard_map/td,fd->tf/dot_general | solution.py:117
  165.3 10.8 %multiply_reduce_fusion.2 = (f32[768]{0:T(1024)}, f32[1024]{0:T(1024)S(1)}, f32[1024,768]{0,1:T(8,128)}) fusion(f32[1024,768]{0,1:T(8,128)S(1)} %get-tuple-element.114, f32[1024]{0:T(1024)S(1)} %fusion.92, f32[768]{0:T(1024)S(1)} %copy-done.37, bf16[1024,3072]{1,0:T(8,128)(2,1)} %fusion.16, bf16[768,3072]{1,0:T(8,128)(2,1)} %param.14), kind=kOutput, calls=%fused_computation.88 | convolution fusion | flops 4836554752 | bytes 17315840 | tf_op jit(solution)/shard_map/tf,df->td/dot_general | solution.py:121
  176.1 15.9 %fusion.42 = (f32[]{:T(128)}, f32[]{:T(128)}, bf16[1,1,1024,768]{2,3,1,0:T(8,128)(2,1)}, f32[1024,768]{0,1:T(8,128)}) fusion(f32[1024,768]{0,1:T(8,128)} %get-tuple-element.146, f32[1024]{0:T(1024)S(1)} %copy-done.48, f32[1024,768]{0,1:T(8,128)S(1)} %get-tuple-element.114, f32[1024]{0:T(1024)S(1)} %multiply_multiply_fusion.5, f32[1024]{0:T(1024)S(1)} %fusion.92, ...), kind=kOutput, calls=%fused_computation.63 | convolution fusion | flops 4871946240 | bytes 33045512 | tf_op jit(solution)/shard_map/dot_general | solution.py:102
  192.1 4.8 fusion.83
  201.8 32.1 %multiply_reduce_fusion.1 = (f32[12,512]{1,0:T(8,128)S(1)}, f32[12,512,2048]{2,1,0:T(8,128)}) fusion(f32[12,512,2048]{2,1,0:T(8,128)} %get-tuple-element.145, f32[12,512]{1,0:T(8,128)S(1)} %copy-done.42, bf16[512,12,64]{0,2,1:T(8,128)(2,1)S(1)} %bitcast.170, bf16[1024,12,64]{0,2,1:T(8,128)(2,1)} %bitcast.9, bf16[1024,12,64]{0,2,1:T(8,128)(2,1)S(1)} %copy-done.26), kind=kOutput, calls=%fused_computation.5 | convolution fusion | flops 1654646784 | bytes 104644608 | tf_op jit(solution)/shard_map/while/body/eval_jaxpr/qhd,khd->hqk/dot_general | solution.py:144
  233.9 40.3 %multiply_convert_fusion.1 = bf16[12,512,2048]{2,1,0:T(8,128)(2,1)} fusion(f32[12,512,2048]{2,1,0:T(8,128)} %get-tuple-element.151, f32[12,512]{1,0:T(8,128)S(1)} %get-tuple-element.150, f32[12,512,2048]{2,1,0:T(8,128)} %get-tuple-element.145, f32[12,512]{1,0:T(8,128)S(1)} %copy-done.42), kind=kLoop, calls=%fused_computation.4 | loop fusion | flops 50331648 | bytes 125878272 | tf_op jit(solution)/shard_map/while/body/eval_jaxpr/convert_element_type | solution.py:148
  274.2 14.0 %multiply_bitcast_fusion.1 = f32[512,12,64]{0,2,1:T(8,128)} fusion(bf16[12,512,2048]{2,1,0:T(8,128)(2,1)} %multiply_convert_fusion.1, bf16[1024,12,64]{0,2,1:T(8,128)(2,1)} %bitcast.16, bf16[1024,12,64]{0,2,1:T(8,128)(2,1)S(1)} %copy-done.9), kind=kOutput, calls=%fused_computation.116 | convolution fusion | flops 1617297408 | bytes 29884416 | tf_op jit(solution)/shard_map/while/body/eval_jaxpr/hqk,khd->qhd/dot_general | solution.py:150
  288.2 15.3 %fusion.110 = f32[12,64,2048]{2,1,0:T(8,128)} fusion(bf16[12,512,2048]{2,1,0:T(8,128)(2,1)} %multiply_convert_fusion.1, bf16[1,1024,12,32]{1,3,2,0:T(8,128)(2,1)S(1)} %copy-done.15, bf16[1,1024,12,32]{1,3,2,0:T(8,128)(2,1)S(1)} %copy-done.17), kind=kOutput, calls=%fused_computation.164 | convolution fusion | flops 1612185600 | bytes 33030144 | tf_op jit(solution)/shard_map/while/body/eval_jaxpr/hqk,qhd->khd/dot_general | solution.py:155
  303.5 20.1 %fusion.17 = f32[12,64,2048]{2,1,0:T(8,128)} fusion(bf16[512,12,64]{0,2,1:T(8,128)(2,1)S(1)} %bitcast.172, f32[12,512,2048]{2,1,0:T(8,128)} %get-tuple-element.143, f32[12,512]{1,0:T(8,128)S(1)} %copy-done.41), kind=kOutput, calls=%fused_computation.30 | convolution fusion | flops 1635778560 | bytes 57434112 | tf_op jit(solution)/shard_map/while/body/eval_jaxpr/hqk,qhd->khd/dot_general | solution.py:160
  323.6 32.3 %multiply_reduce_fusion = (f32[12,512]{1,0:T(8,128)S(1)}, f32[12,512,2048]{2,1,0:T(8,128)}) fusion(f32[12,512,2048]{2,1,0:T(8,128)} %get-tuple-element.143, f32[12,512]{1,0:T(8,128)S(1)} %copy-done.41, bf16[512,12,64]{0,2,1:T(8,128)(2,1)S(1)} %bitcast.173, bf16[1024,12,64]{0,2,1:T(8,128)(2,1)} %bitcast.9, bf16[1024,12,64]{0,2,1:T(8,128)(2,1)S(1)} %copy-done.27), kind=kOutput, calls=%fused_computation.3 | convolution fusion | flops 1654646784 | bytes 104644608 | tf_op jit(solution)/shard_map/while/body/eval_jaxpr/qhd,khd->hqk/dot_general | solution.py:144
  355.9 22.6 %fusion.36 = f32[12,64,2048]{2,1,0:T(8,128)} fusion(f32[12,64,2048]{2,1,0:T(8,128)} %fusion.17, bf16[512,12,64]{0,2,1:T(8,128)(2,1)S(1)} %bitcast.171, f32[12,512,2048]{2,1,0:T(8,128)} %get-tuple-element.145, f32[12,512]{1,0:T(8,128)S(1)} %copy-done.43), kind=kOutput, calls=%fused_computation.59 | convolution fusion | flops 1637351424 | bytes 63725568 | tf_op jit(solution)/shard_map/while/body/eval_jaxpr/hqk,qhd->khd/dot_general | solution.py:160
  383.2 40.9 %multiply_convert_fusion = bf16[12,512,2048]{2,1,0:T(8,128)(2,1)} fusion(f32[12,512,2048]{2,1,0:T(8,128)} %get-tuple-element.149, f32[12,512]{1,0:T(8,128)S(1)} %get-tuple-element.148, f32[12,512,2048]{2,1,0:T(8,128)} %get-tuple-element.143, f32[12,512]{1,0:T(8,128)S(1)} %copy-done.41), kind=kLoop, calls=%fused_computation.2 | loop fusion | flops 50331648 | bytes 125878272 | tf_op jit(solution)/shard_map/while/body/eval_jaxpr/convert_element_type | solution.py:148
  424.1 14.6 %add_multiply_fusion = f32[12,64,2048]{2,1,0:T(8,128)S(1)} fusion(f32[12,64,2048]{2,1,0:T(8,128)} %fusion.110, bf16[12,512,2048]{2,1,0:T(8,128)(2,1)} %multiply_convert_fusion, bf16[1,1024,12,32]{1,3,2,0:T(8,128)(2,1)S(1)} %copy-done.18, bf16[1,1024,12,32]{1,3,2,0:T(8,128)(2,1)S(1)} %copy-done.16), kind=kOutput, calls=%fused_computation.39 | convolution fusion | flops 1615331328 | bytes 39321600 | tf_op jit(solution)/shard_map/while/body/eval_jaxpr/hqk,qhd->khd/dot_general | solution.py:155
  444.0 14.1 %multiply_bitcast_fusion = f32[512,12,64]{0,2,1:T(8,128)} fusion(bf16[12,512,2048]{2,1,0:T(8,128)(2,1)} %multiply_convert_fusion, bf16[1024,12,64]{0,2,1:T(8,128)(2,1)} %bitcast.16, bf16[1024,12,64]{0,2,1:T(8,128)(2,1)S(1)} %copy-done.10), kind=kOutput, calls=%fused_computation.115 | convolution fusion | flops 1617297408 | bytes 29884416 | tf_op jit(solution)/shard_map/while/body/eval_jaxpr/hqk,khd->qhd/dot_general | solution.py:150
  470.7 6.1 fusion.56
  477.5 10.7 %fusion.100 = f32[768,3072]{0,1:T(8,128)} fusion(bf16[1024,3072]{1,0:T(8,128)(2,1)} %fusion.16, f32[1024,768]{0,1:T(8,128)} %copy-done.5, f32[768]{0:T(1024)S(1)} %copy-done.38, f32[1024]{0:T(1024)S(1)} %copy-done.36), kind=kOutput, calls=%fused_computation.162 | convolution fusion | flops 4834197504 | bytes 18881536 | tf_op jit(solution)/shard_map/td,tf->df/dot_general | solution.py:120
  488.3 13.3 %fusion.61 = f32[3072,768]{1,0:T(8,128)} fusion(bf16[1,1,1024,768]{3,2,1,0:T(8,128)(2,1)} %param.11, f32[1024,3072]{1,0:T(8,128)} %copy-done.11), kind=kOutput, calls=%fused_computation.106 | convolution fusion | flops 4860149760 | bytes 23592960 | tf_op jit(solution)/shard_map/tf,td->fd/dot_general | solution.py:116
  504.2 8.5 fusion.47
  519.4 44.9 %all-reduce = (f32[768]{0:T(1024)}, f32[768]{0:T(1024)}, f32[3]{0:T(128)S(1)}, f32[]{:T(128)}) all-reduce(f32[768]{0:T(1024)S(1)} %get-tuple-element.104, f32[768]{0:T(1024)S(1)} %copy-done.50, f32[3]{0:T(128)S(1)} %pad_maximum_fusion.4, f32[]{:T(128)S(6)} %convert_element_type.226), channel_id=1, replica_groups=mesh['stream'=2,'batch'=16] {'stream','batch'}, use_global_device_ids=true, to_apply=%region_15.16 | all-reduce | flops 1540 | bytes 12320 | tf_op jit(solution)/shard_map/psum | solution.py:185
  565.5 36.3 %reduce-scatter.5.cloned.1.call-done = f32[24,2304]{1,0:T(8,128)} async-done(((f32[768,2304]{1,0:T(8,128)}), f32[24,2304]{1,0:T(8,128)}) %reduce-scatter.5.cloned.1.call-update) | async-done | bytes 221200 | tf_op jit(solution)/shard_map/reduce_scatter | solution.py:187
  601.7 141.3 %reduce-scatter.9.cloned.1.call-done = f32[768,96]{0,1:T(8,128)} async-done(((f32[768,3072]{0,1:T(8,128)}), f32[768,96]{0,1:T(8,128)}) %reduce-scatter.9.cloned.1.call-update) | async-done | bytes 294928 | tf_op jit(solution)/shard_map/reduce_scatter | solution.py:189
  743.1 142.2 %reduce-scatter.11.cloned.1.call-done = f32[96,768]{1,0:T(8,128)} async-done(((f32[3072,768]{1,0:T(8,128)}), f32[96,768]{1,0:T(8,128)}) %reduce-scatter.11.cloned.1.call-update) | async-done | bytes 294928 | tf_op jit(solution)/shard_map/reduce_scatter | solution.py:190
  (161 shorter events, 62.3 us)
Async XLA Ops:
  7.2 130.7 %copy-start = (bf16[768,768]{1,0:T(8,128)(2,1)S(1)}, bf16[768,768]{1,0:T(8,128)(2,1)}, u32[]{:S(2)}) copy-start(bf16[768,768]{1,0:T(8,128)(2,1)} %param.13) | copy-start | bytes 3538948
  7.2 558.3 %reduce-scatter.7.cloned.1.call-start = ((), (), s32[]{:S(2)}) async-start(), calls=%async_computation.5 | async-start | bytes 2433024 | tf_op jit(solution)/shard_map/reduce_scatter | solution.py:188
  8.5 17.8 %copy-start.22 = (f32[1024,32]{0,1:T(8,128)}, f32[1024,32]{0,1:T(8,128)S(1)}, u32[]{:S(2)}) copy-start(f32[1024,32]{0,1:T(8,128)S(1)} %get-tuple-element.141) | copy-start | bytes 393220
  8.5 17.8 %copy-start.28 = (f32[1024,32]{0,1:T(8,128)}, f32[1024,32]{0,1:T(8,128)S(1)}, u32[]{:S(2)}) copy-start(f32[1024,32]{0,1:T(8,128)S(1)} %get-tuple-element.140) | copy-start | bytes 393220
  28.3 21.4 %collective-permute-start.1 = (bf16[1,1024,768]{1,2,0:T(8,128)(2,1)}, bf16[1,1024,768]{1,2,0:T(8,128)(2,1)}, u32[]{:S(2)}, u32[]{:S(2)}) collective-permute-start(bf16[1,1024,768]{1,2,0:T(8,128)(2,1)} %bitcast.15), channel_id=1, source_target_pairs={{0,16},{1,17},{2,18},{3,19},{4,20},{5,21},{6,22},{7,23},{8,24},{9,... | collective-permute-start | bytes 4718600 | tf_op jit(solution)/shard_map/ppermute | solution.py:18
  33.2 64.4 %collective-permute-start = (bf16[1,1024,768]{1,2,0:T(8,128)(2,1)}, bf16[1,1024,768]{1,2,0:T(8,128)(2,1)}, u32[]{:S(2)}, u32[]{:S(2)}) collective-permute-start(bf16[1,1024,768]{1,2,0:T(8,128)(2,1)} %bitcast.8), channel_id=1, source_target_pairs={{0,16},{1,17},{2,18},{3,19},{4,20},{5,21},{6,22},{7,23},{8,24},{9,... | collective-permute-start | bytes 4718600 | tf_op jit(solution)/shard_map/ppermute | solution.py:18
  36.4 37.3 %copy-start.8 = (bf16[1024,12,64]{0,2,1:T(8,128)(2,1)}, bf16[1024,12,64]{0,2,1:T(8,128)(2,1)S(1)}, u32[]{:S(2)}) copy-start(bf16[1024,12,64]{0,2,1:T(8,128)(2,1)S(1)} %fusion.127) | copy-start | bytes 4718596
  46.1 27.6 %copy-start.14 = (bf16[1,1024,12,32]{1,3,2,0:T(8,128)(2,1)}, bf16[1,1024,12,32]{1,3,2,0:T(8,128)(2,1)S(1)}, u32[]{:S(2)}) copy-start(bf16[1,1024,12,32]{1,3,2,0:T(8,128)(2,1)S(1)} %get-tuple-element.123) | copy-start | bytes 2359300
  97.6 19.5 %copy-start.25 = (bf16[1024,12,64]{0,2,1:T(8,128)(2,1)S(1)}, bf16[1024,12,64]{0,2,1:T(8,128)(2,1)}, u32[]{:S(2)}) copy-start(bf16[1024,12,64]{0,2,1:T(8,128)(2,1)} %slice_bitcast_fusion.2) | copy-start | bytes 4718596
  97.6 19.5 %copy-start.42 = (f32[12,512]{1,0:T(8,128)S(1)}, f32[12,512]{1,0:T(8,128)}, u32[]{:S(2)}) copy-start(f32[12,512]{1,0:T(8,128)} %get-tuple-element.144) | copy-start | bytes 73732
  141.5 34.6 %copy-start.5 = (f32[1024,768]{0,1:T(8,128)}, f32[1024,768]{0,1:T(8,128)S(1)}, u32[]{:S(2)}) copy-start(f32[1024,768]{0,1:T(8,128)S(1)} %get-tuple-element.114) | copy-start | bytes 9437188
  141.5 34.6 %copy-start.35 = (f32[1024]{0:T(1024)}, f32[1024]{0:T(1024)S(1)}, u32[]{:S(2)}) copy-start(f32[1024]{0:T(1024)S(1)} %fusion.92) | copy-start | bytes 12292
  146.8 18.5 %copy-start.11 = (f32[1024,3072]{1,0:T(8,128)}, f32[1024,3072]{1,0:T(8,128)S(1)}, u32[]{:S(2)}) copy-start(f32[1024,3072]{1,0:T(8,128)S(1)} %fusion.101) | copy-start | bytes 37748740
  165.3 10.8 %copy-start.48 = (f32[1024]{0:T(1024)S(1)}, f32[1024]{0:T(1024)}, u32[]{:S(2)}) copy-start(f32[1024]{0:T(1024)} %get-tuple-element.154) | copy-start | bytes 12292
  201.1 32.8 %copy-start.30 = (bf16[512,768]{0,1:T(8,128)(2,1)}, bf16[512,768]{0,1:T(8,128)(2,1)S(1)}, u32[]{:S(2)}) copy-start(bf16[512,768]{0,1:T(8,128)(2,1)S(1)} %get-tuple-element.127) | copy-start | bytes 2359300
  233.9 40.3 %copy-start.9 = (bf16[1024,12,64]{0,2,1:T(8,128)(2,1)S(1)}, bf16[1024,12,64]{0,2,1:T(8,128)(2,1)}, u32[]{:S(2)}) copy-start(bf16[1024,12,64]{0,2,1:T(8,128)(2,1)} %copy-done.8) | copy-start | bytes 4718596
  274.2 14.0 %copy-start.15 = (bf16[1,1024,12,32]{1,3,2,0:T(8,128)(2,1)S(1)}, bf16[1,1024,12,32]{1,3,2,0:T(8,128)(2,1)}, u32[]{:S(2)}) copy-start(bf16[1,1024,12,32]{1,3,2,0:T(8,128)(2,1)} %copy-done.14) | copy-start | bytes 2359300
  274.2 14.0 %copy-start.17 = (bf16[1,1024,12,32]{1,3,2,0:T(8,128)(2,1)S(1)}, bf16[1,1024,12,32]{1,3,2,0:T(8,128)(2,1)}, u32[]{:S(2)}) copy-start(bf16[1,1024,12,32]{1,3,2,0:T(8,128)(2,1)} %get-tuple-element.124) | copy-start | bytes 2359300
  288.2 15.3 %copy-start.32 = (bf16[512,768]{0,1:T(8,128)(2,1)S(1)}, bf16[512,768]{0,1:T(8,128)(2,1)}, u32[]{:S(2)}) copy-start(bf16[512,768]{0,1:T(8,128)(2,1)} %get-tuple-element.128) | copy-start | bytes 2359300
  288.2 15.3 %copy-start.41 = (f32[12,512]{1,0:T(8,128)S(1)}, f32[12,512]{1,0:T(8,128)}, u32[]{:S(2)}) copy-start(f32[12,512]{1,0:T(8,128)} %get-tuple-element.142) | copy-start | bytes 73732
  303.5 20.1 %copy-start.27 = (bf16[1024,12,64]{0,2,1:T(8,128)(2,1)S(1)}, bf16[1024,12,64]{0,2,1:T(8,128)(2,1)}, u32[]{:S(2)}) copy-start(bf16[1024,12,64]{0,2,1:T(8,128)(2,1)} %slice_bitcast_fusion.2) | copy-start | bytes 4718596
  303.5 20.1 %copy-start.33 = (bf16[512,768]{0,1:T(8,128)(2,1)S(1)}, bf16[512,768]{0,1:T(8,128)(2,1)}, u32[]{:S(2)}) copy-start(bf16[512,768]{0,1:T(8,128)(2,1)} %get-tuple-element.128) | copy-start | bytes 2359300
  323.5 32.4 %copy-start.31 = (bf16[512,768]{0,1:T(8,128)(2,1)S(1)}, bf16[512,768]{0,1:T(8,128)(2,1)}, u32[]{:S(2)}) copy-start(bf16[512,768]{0,1:T(8,128)(2,1)} %copy-done.30) | copy-start | bytes 2359300
  323.5 32.4 %copy-start.43 = (f32[12,512]{1,0:T(8,128)S(1)}, f32[12,512]{1,0:T(8,128)}, u32[]{:S(2)}) copy-start(f32[12,512]{1,0:T(8,128)} %get-tuple-element.144) | copy-start | bytes 73732
  355.9 245.9 %reduce-scatter.5.cloned.1.call-start = ((), (), s32[]{:S(2)}) async-start(), calls=%async_computation.4 | async-start | bytes 7299072 | tf_op jit(solution)/shard_map/reduce_scatter | solution.py:187
  381.8 83.6 %collective-permute-start.3 = (bf16[1,1024,768]{1,2,0:T(8,128)(2,1)}, bf16[1,1024,768]{1,2,0:T(8,128)(2,1)}, u32[]{:S(2)}, u32[]{:S(2)}) collective-permute-start(bf16[1,1024,768]{1,2,0:T(8,128)(2,1)} %slice.192), channel_id=1, source_target_pairs={{16,0},{17,1},{18,2},{19,3},{20,4},{21,5},{22,6},{23,7},{24,8},{25... | collective-permute-start | bytes 4718600 | tf_op jit(solution)/shard_map/ppermute | solution.py:18
  383.1 41.0 %copy-start.16 = (bf16[1,1024,12,32]{1,3,2,0:T(8,128)(2,1)S(1)}, bf16[1,1024,12,32]{1,3,2,0:T(8,128)(2,1)}, u32[]{:S(2)}) copy-start(bf16[1,1024,12,32]{1,3,2,0:T(8,128)(2,1)} %copy-done.14) | copy-start | bytes 2359300
  383.1 41.0 %copy-start.18 = (bf16[1,1024,12,32]{1,3,2,0:T(8,128)(2,1)S(1)}, bf16[1,1024,12,32]{1,3,2,0:T(8,128)(2,1)}, u32[]{:S(2)}) copy-start(bf16[1,1024,12,32]{1,3,2,0:T(8,128)(2,1)} %get-tuple-element.124) | copy-start | bytes 2359300
  442.8 17.8 %collective-permute-start.2 = (bf16[1,1024,768]{1,2,0:T(8,128)(2,1)}, bf16[1,1024,768]{1,2,0:T(8,128)(2,1)}, u32[]{:S(2)}, u32[]{:S(2)}) collective-permute-start(bf16[1,1024,768]{1,2,0:T(8,128)(2,1)} %slice.193), channel_id=1, source_target_pairs={{16,0},{17,1},{18,2},{19,3},{20,4},{21,5},{22,6},{23,7},{24,8},{25... | collective-permute-start | bytes 4718600 | tf_op jit(solution)/shard_map/ppermute | solution.py:18
  476.8 266.2 %reduce-scatter.9.cloned.1.call-start = ((), (), s32[]{:S(2)}) async-start(), calls=%async_computation.6 | async-start | bytes 9732096 | tf_op jit(solution)/shard_map/reduce_scatter | solution.py:189
  488.2 397.0 %reduce-scatter.11.cloned.1.call-start = ((), (), s32[]{:S(2)}) async-start(), calls=%async_computation.7 | async-start | bytes 9732096 | tf_op jit(solution)/shard_map/reduce_scatter | solution.py:190
  512.8 372.5 %copy-start.1 = (bf16[768,768]{1,0:T(8,128)(2,1)S(1)}, bf16[768,768]{1,0:T(8,128)(2,1)}, u32[]{:S(2)}) copy-start(bf16[768,768]{1,0:T(8,128)(2,1)} %param.13) | copy-start | bytes 3538948
  (29 other events, 111.5 us)
Sparse Core Ops, SparseCore 0:
  356.0 102.6 reduce-scatter.6
  477.0 124.7 reduce-scatter.4
  608.2 134.7 reduce-scatter.8
  750.4 134.7 reduce-scatter.10
where the time goes:
time: 898 us; the launch traced here: 892 us
  matrix products  358 us (40%)
  waiting for transfers between devices  320 us (36%)
  other arithmetic  106 us (12%)
  blocking collectives  44.9 us (5%)
  local copies, waits for them, and re-layouts  37.9 us (4%)
  between operations  15.9 us (2%)
  starting transfers between devices  9.23 us (1%)
    reduce_scatter x1, waiting for transfers between devices, on_device(): lax.psum_scatter(down_grad, ('stream', 'batch'), scatter_dimension=0, til...  142 us
    reduce_scatter x1, waiting for transfers between devices, on_device(): lax.psum_scatter(up_grad, ('stream', 'batch'), scatter_dimension=1, tiled...  141 us
    convert_element_type x2, other arithmetic, backward_row(): grad_scores = grad_scores.astype(jnp.bfloat16)  81.2 us
    dot_general x2, matrix products, backward_row(): jnp.einsum('qhd,khd->hqk', g_part, v_row, preferred_element_type=jnp.floa...  64.3 us
    sub x2, matrix products, forward_row(): expo = jnp.exp(scores - top)  47.9 us
    psum x1, blocking collectives, on_device(): lax.psum((attn_gain_grad, mlp_gain_grad), ('stream', 'batch'))  44.9 us
    dot_general x2, matrix products, backward_row(): jnp.einsum('hqk,qhd->khd', low_prob, g_part, preferred_element_type=jnp.f...  42.7 us
    dot_general x2, matrix products, forward_row(): jnp.einsum('hqk,khd->qhd', prob, v_row, preferred_element_type=jnp.float32)  38.8 us
  transfers between devices with their start and end apart: 8, of which 3 were waited for; matrix products, arithmetic and copies ran while one was open for 24% of the time, Pallas kernels for 0%

commit v1 on v0

v1 whole, which is shorter than its diff:
```python
import functools

import jax
import jax.numpy as jnp
import numpy as np
from jax import lax
from jax.experimental import pallas as pl
from jax.experimental.pallas import tpu as pltpu
from jax.sharding import PartitionSpec as P

f32 = jnp.float32
bf16 = jnp.bfloat16

HD = 64
BLK = 16
EPS = 1e-06
NEG = -1e30
PW = 2 * HD
T = 128
R = 256
FC = 256
SCALE = HD**-0.5
GROUPS = 3

SMEM = pl.BlockSpec(memory_space=pltpu.SMEM)


def params(mib):
    return pltpu.CompilerParams(vmem_limit_bytes=mib << 20)


def shape(dims, dtype):
    return jax.ShapeDtypeStruct(dims, dtype)


def nn(a, b):
    return jnp.dot(a, b, preferred_element_type=f32)


def nt(a, b):
    return lax.dot_general(a, b, (((1,), (1,)), ((), ())), preferred_element_type=f32)


def tn(a, b):
    return lax.dot_general(a, b, (((0,), (0,)), ((), ())), preferred_element_type=f32)


def whole(dims):
    return pl.BlockSpec(dims, lambda *_: (0,) * len(dims), pipeline_mode=pl.Buffered(1))


def inv_rms(v):
    return lax.rsqrt(jnp.mean(v * v, axis=-1, keepdims=True) + EPS)


def norm_back(v, gain, grad):
    r = inv_rms(v)
    unit = v * r
    scaled = grad * gain
    inner = jnp.mean(scaled * unit, axis=-1, keepdims=True)
    return r * (scaled - unit * inner), grad * unit


def rotary_tables(length):
    half = HD // 2
    freqs = np.exp(-np.log(10000.0) * np.arange(half) / half).astype(np.float32)
    angles = (np.arange(length, dtype=np.float32)[:, None] * freqs[None, :]).astype(np.float64)
    cosine, sine = np.cos(angles), np.sin(angles)
    zero = np.zeros_like(sine)
    pair = lambda a, b: np.concatenate([a, b, a, b], axis=1).astype(np.float32)
    return pair(cosine, cosine), pair(-sine, zero), pair(zero, sine)


def rotated(v, cosine, minus, plus, sign):
    outs = []
    for c in range(0, v.shape[1], PW):
        part = v[:, c : c + PW]
        ahead = pltpu.roll(part, PW - HD // 2, 1)
        behind = pltpu.roll(part, HD // 2, 1)
        outs.append(part * cosine + (ahead * minus + behind * plus) * sign)
    return jnp.concatenate(outs, axis=1)


def token_weight(start, length, rows):
    return lax.broadcasted_iota(jnp.int32, (rows, 1), 0) + start < length


def row_sum(v):
    return jnp.sum(v, axis=0, keepdims=True)


def project_kernel(info, x, gain, wq, wk, wv, cosine, minus, plus, q, k, v, h1t, sums):
    at = pl.program_id(0)

    @pl.when(at == 0)
    def _():
        sums[...] = jnp.zeros_like(sums)

    value = x[...].astype(f32)
    h1 = (value * inv_rms(value) * gain[...]).astype(bf16)
    tables = (cosine[...], minus[...], plus[...], 1.0)
    q[...] = rotated(nn(h1, wq[...]), *tables).astype(bf16)
    k[...] = rotated(nn(h1, wk[...]), *tables).astype(bf16)
    v[...] = nn(h1, wv[...]).astype(bf16)
    h1t[...] = h1.T
    weight = token_weight(at * R, info[1], R)
    sums[0:1, :] += row_sum(jnp.where(weight, value * value, 0.0))


def project(info, x, gain, weight, tables):
    seq, width = x.shape
    rows = pl.BlockSpec((R, width), lambda i: (i, 0))
    table = pl.BlockSpec((R, PW), lambda i: (i, 0))
    third = lambda c: pl.BlockSpec((width, width), lambda i: (0, c), pipeline_mode=pl.Buffered(1))
    return pl.pallas_call(
        project_kernel,
        grid=(seq // R,),
        in_specs=[SMEM, rows, whole((1, width)), third(0), third(1), third(2), table, table, table],
        out_specs=[rows, rows, rows, pl.BlockSpec((width, R), lambda i: (0, i)), whole((8, width))],
        out_shape=[shape((seq, width), bf16)] * 3 + [shape((width, seq), bf16), shape((8, width), f32)],
        compiler_params=params(40),
        cost_estimate=pl.CostEstimate(
            flops=2 * seq * width * 3 * width, bytes_accessed=12 * seq * width, transcendentals=0
        ),
        name="project",
    )(info, x, gain, weight, weight, weight, *tables)


def clean_kv_kernel(info, x, received, gain, wk, wv, cosine, minus, plus, k, v):
    value = jnp.where(info[0] == 1, received[...].astype(f32), x[...].astype(f32))
    h1 = (value * inv_rms(value) * gain[...]).astype(bf16)
    k[...] = rotated(nn(h1, wk[...]), cosine[...], minus[...], plus[...], 1.0).astype(bf16)
    v[...] = nn(h1, wv[...]).astype(bf16)


def clean_kv(info, x, received, gain, weight, tables):
    seq, width = x.shape
    rows = pl.BlockSpec((R, width), lambda i: (i, 0))
    table = pl.BlockSpec((R, PW), lambda i: (i, 0))
    third = lambda c: pl.BlockSpec((width, width), lambda i: (0, c), pipeline_mode=pl.Buffered(1))
    return pl.pallas_call(
        clean_kv_kernel,
        grid=(seq // R,),
        in_specs=[SMEM, rows, rows, whole((1, width)), third(1), third(2), table, table, table],
        out_specs=[rows, rows],
        out_shape=[shape((seq, width), bf16)] * 2,
        compiler_params=params(40),
        cost_estimate=pl.CostEstimate(
            flops=2 * seq * width * 2 * width, bytes_accessed=10 * seq * width, transcendentals=0
        ),
        name="clean_kv",
    )(info, x, received, gain, weight, weight, *tables)


def stacked(tile, low):
    zero = jnp.zeros_like(tile)
    return jnp.concatenate([jnp.where(low, tile, zero), jnp.where(low, zero, tile)], axis=0)


def unstacked(tile_t):
    half = lax.broadcasted_iota(jnp.int32, (PW, 1), 0) < HD
    return jnp.where(half, tile_t[:, :T], tile_t[:, T:])


def chunks_of(i):
    out, j = [], 0
    while j < i:
        n = 2 if i - j >= 2 else 1
        out.append((j * T, n * T))
        j += n
    return out


def edge_masks(noisy):
    row = lax.broadcasted_iota(jnp.int32, (T, 2 * T), 0) // BLK
    col = (lax.broadcasted_iota(jnp.int32, (T, 2 * T), 1) % T) // BLK
    own = jnp.logical_or(row == col, jnp.logical_and(row < col, noisy == 0))
    other = jnp.logical_and(row < col, noisy == 1)
    return own, other


def masked(s, start, length):
    pos = lax.broadcasted_iota(jnp.int32, s.shape, 0) + start
    return jnp.where(pos < length, s, NEG)


def over_rows(op, v):
    return op(v.reshape(v.shape[0] // 8, 8, v.shape[1]), axis=0)


def attend_kernel(info, q, ko, vo, kc, vc, o, o_t, lse, vo_t, vc_t, scores):
    noisy, length = info[0], info[1]
    seq = q.shape[0]
    low = lax.broadcasted_iota(jnp.int32, (1, PW), 1) < HD
    own_mask, other_mask = edge_masks(noisy)
    vo_t[...] = vo[...].T
    vc_t[...] = vc[...].T
    for i in range(seq // T):
        at = pl.ds(i * T, T)
        q2 = stacked(q[at, :] * bf16(SCALE), low)
        buf = scores.at[i % 2]
        edge = nt(jnp.concatenate([ko[at, :], kc[at, :]], 0), q2)
        own = masked(jnp.where(own_mask, edge[:T], NEG), i * T, length)
        other = masked(jnp.where(other_mask, edge[T:], NEG), i * T, length)
        buf[pl.ds(0, T), :] = own
        buf[pl.ds(T, T), :] = other
        top = over_rows(jnp.max, jnp.maximum(own, other))
        for start, size in chunks_of(i):
            s = masked(nt(kc[pl.ds(start, size), :], q2), start, length)
            buf[pl.ds(2 * T + start, size), :] = s
            top = jnp.maximum(top, over_rows(jnp.max, s))
        top = jnp.max(top, axis=0, keepdims=True)
        p = jnp.exp(buf[pl.ds(0, 2 * T), :] - top)
        total = over_rows(jnp.sum, p)
        acc = nn(jnp.concatenate([vo_t[:, at], vc_t[:, at]], 1), p.astype(bf16))
        for start, size in chunks_of(i):
            p = jnp.exp(buf[pl.ds(2 * T + start, size), :] - top)
            total = total + over_rows(jnp.sum, p)
            acc = acc + nn(vc_t[:, pl.ds(start, size)], p.astype(bf16))
        total = row_sum(total)
        lse[0, pl.ds(i, 1), :] = top + jnp.log(total)
        out_t = unstacked(acc / total)
        o_t[:, at] = out_t.astype(bf16)
        o[at, :] = out_t.T.astype(bf16)


def attend(info, q, ko, vo, kc, vc):
    seq, width = q.shape
    pairs = width // PW
    cols = pl.BlockSpec((seq, PW), lambda h: (0, h))
    rows = pl.BlockSpec((PW, seq), lambda h: (h, 0))
    return pl.pallas_call(
        attend_kernel,
        grid=(pairs,),
        in_specs=[SMEM] + [cols] * 5,
        out_specs=[cols, rows, pl.BlockSpec((1, seq // T, 2 * T), lambda h: (h, 0, 0))],
        out_shape=[shape((seq, width), bf16), shape((width, seq), bf16), shape((pairs, seq // T, 2 * T), f32)],
        scratch_shapes=[
            pltpu.VMEM((PW, seq), bf16),
            pltpu.VMEM((PW, seq), bf16),
            pltpu.VMEM((2, seq + T, 2 * T), f32),
        ],
        compiler_params=params(40),
        cost_estimate=pl.CostEstimate(
            flops=4 * seq * seq * width, bytes_accessed=14 * seq * width, transcendentals=seq * seq * 8
        ),
        name="attend",
    )(info, q, ko, vo, kc, vc)


def attend_back_kernel(
    info, q, ko, vo, kc, vc, o, do, lse, dq, dko, dvo, dkc, dvc, ko_t, kc_t, dk_acc, dv_acc
):
    noisy, length = info[0], info[1]
    seq = q.shape[0]
    low = lax.broadcasted_iota(jnp.int32, (1, PW), 1) < HD
    own_mask, other_mask = edge_masks(noisy)
    ko_t[...] = ko[...].T
    kc_t[...] = kc[...].T
    for i in range(seq // T):
        at = pl.ds(i * T, T)
        q2 = stacked(q[at, :] * bf16(SCALE), low)
        do2 = stacked(do[at, :], low)
        prod = (do[at, :].astype(f32) * o[at, :].astype(f32)).T
        delta = jnp.concatenate([row_sum(prod[:HD]), row_sum(prod[HD:])], 1)
        norm = lse[0, pl.ds(i, 1), :]
        s = nt(jnp.concatenate([ko[at, :], kc[at, :]], 0), q2)
        own = masked(jnp.where(own_mask, s[:T], NEG), i * T, length)
        other = masked(jnp.where(other_mask, s[T:], NEG), i * T, length)
        p = jnp.exp(jnp.concatenate([own, other], 0) - norm)
        dp = nt(jnp.concatenate([vo[at, :], vc[at, :]], 0), do2)
        ds = (p * (dp - delta)).astype(bf16)
        dv = nn(p.astype(bf16), do2)
        dk = nn(ds, q2)
        dvo[at, :] = dv[:T]
        dko[at, :] = dk[:T]
        dv_acc[at, :] = dv[T:]
        dk_acc[at, :] = dk[T:]
        dq_t = nn(jnp.concatenate([ko_t[:, at], kc_t[:, at]], 1), ds)
        for start, size in chunks_of(i):
            rows = pl.ds(start, size)
            p = jnp.exp(masked(nt(kc[rows, :], q2), start, length) - norm)
            ds = (p * (nt(vc[rows, :], do2) - delta)).astype(bf16)
            dv_acc[rows, :] += nn(p.astype(bf16), do2)
            dk_acc[rows, :] += nn(ds, q2)
            dq_t = dq_t + nn(kc_t[:, rows], ds)
        dq[at, :] = unstacked(dq_t).T * SCALE
    dkc[...] = dk_acc[...].astype(dkc.dtype)
    dvc[...] = dv_acc[...].astype(dvc.dtype)


def attend_back(info, q, ko, vo, kc, vc, o, do, lse):
    seq, width = q.shape
    pairs = width // PW
    cols = pl.BlockSpec((seq, PW), lambda h: (0, h))
    return pl.pallas_call(
        attend_back_kernel,
        grid=(pairs,),
        in_specs=[SMEM] + [cols] * 7 + [pl.BlockSpec((1, seq // T, 2 * T), lambda h: (h, 0, 0))],
        out_specs=[cols] * 5,
        out_shape=[shape((seq, width), f32)] * 3 + [shape((seq, width), bf16)] * 2,
        scratch_shapes=[pltpu.VMEM((PW, seq), bf16)] * 2 + [pltpu.VMEM((seq, PW), f32)] * 2,
        compiler_params=params(40),
        cost_estimate=pl.CostEstimate(
            flops=8 * seq * seq * width, bytes_accessed=30 * seq * width, transcendentals=seq * seq * 8
        ),
        name="attend_back",
    )(info, q, ko, vo, kc, vc, o, do, lse)


def join_kernel(info, x, o, wo, gain, x2, h2, sums):
    at = pl.program_id(0)

    @pl.when(at == 0)
    def _():
        sums[...] = jnp.zeros_like(sums)

    branch = nn(o[...], wo[...])
    value = x[...].astype(f32) + branch
    x2[...] = value
    h2[...] = (value * inv_rms(value) * gain[...]).astype(bf16)
    weight = token_weight(at * R, info[1], R)
    sums[0:1, :] += row_sum(jnp.where(weight, branch * branch, 0.0))


def join(info, x, o, weight, gain):
    seq, width = x.shape
    rows = pl.BlockSpec((R, width), lambda i: (i, 0))
    return pl.pallas_call(
        join_kernel,
        grid=(seq // R,),
        in_specs=[SMEM, rows, rows, whole((width, width)), whole((1, width))],
        out_specs=[rows, rows, whole((8, width))],
        out_shape=[shape((seq, width), f32), shape((seq, width), bf16), shape((8, width), f32)],
        compiler_params=params(40),
        cost_estimate=pl.CostEstimate(
            flops=2 * seq * width * width, bytes_accessed=10 * seq * width, transcendentals=0
        ),
        name="join",
    )(info, x, o, weight, gain)


C0 = 0.7978845608028654
C1 = C0 * 0.044715


def feed_kernel(first, at, h2, dm, w1, w2, m_in, dh_in, m, dh, g_up, g_down, act_s, du_s):
    step = pl.program_id(0)

    @pl.when(step == 0)
    def _():
        if first:
            m[...] = jnp.zeros_like(m)
            dh[...] = jnp.zeros_like(dh)
        else:
            m[...] = m_in[...]
            dh[...] = dh_in[...]

    for t in range(0, h2.shape[0], R):
        rows = pl.ds(t, R)
        u = nn(h2[rows, :], w1[...])
        da = nt(dm[rows, :], w2[...])
        sq = u * u
        half = 0.5 * jnp.tanh(u * (C0 + C1 * sq)) + 0.5
        act = (u * half).astype(bf16)
        slope = half + u * (2.0 * half * (1.0 - half)) * (C0 + 3.0 * C1 * sq)
        du = (da * slope).astype(bf16)
        act_s[rows, :] = act
        du_s[rows, :] = du
        m[rows, :] += nn(act, w2[...])
        dh[rows, :] += nt(du, w1[...])
    g_down[...] = tn(act_s[...], dm[...]).astype(bf16)
    g_up[...] = tn(du_s[...], h2[...]).astype(bf16)


def feed(first, part, h2, dm, w1, w2, m_in, dh_in):
    seq, width = h2.shape
    hidden = w1.shape[1] // 2
    steps = hidden // FC
    held = whole((seq, width))
    grads = pl.BlockSpec((FC, width), lambda c, at: (c, 0))
    carried = [pl.BlockSpec(memory_space=pl.ANY)] * 2 if first else [held] * 2
    return pl.pallas_call(
        functools.partial(feed_kernel, first),
        grid_spec=pltpu.PrefetchScalarGridSpec(
            num_scalar_prefetch=1,
            grid=(steps,),
            in_specs=[
                held,
                held,
                pl.BlockSpec((width, FC), lambda c, at: (0, at[0] * steps + c)),
                pl.BlockSpec((FC, width), lambda c, at: (at[0] * steps + c, 0)),
            ]
            + carried,
            out_specs=[held, held, grads, grads],
            scratch_shapes=[pltpu.VMEM((seq, FC), bf16)] * 2,
        ),
        out_shape=[shape((seq, width), f32)] * 2 + [shape((hidden, width), bf16)] * 2,
        compiler_params=params(56),
        cost_estimate=pl.CostEstimate(
            flops=12 * seq * width * hidden, bytes_accessed=24 * seq * width, transcendentals=seq * hidden
        ),
        name="feed",
    )(part, h2, dm, w1, w2, m_in, dh_in)


def middle_kernel(info, x2, m, dh, dy, o_t, wo, gain, out, dx2, do, g_send, g_keep, sums, acc):
    at = pl.program_id(0)

    @pl.when(at == 0)
    def _():
        sums[...] = jnp.zeros_like(sums)
        acc[...] = jnp.zeros_like(acc)

    value = x2[...]
    mixed = m[...]
    out[...] = (value + mixed).astype(bf16)
    weight = token_weight(at * R, info[1], R)
    sums[0:1, :] += row_sum(jnp.where(weight, mixed * mixed, 0.0))
    grad, gain_terms = norm_back(value, gain[...], dh[...])
    sums[1:2, :] += row_sum(gain_terms)
    grad = grad + dy[...].astype(f32)
    dx2[...] = grad
    da = grad.astype(bf16)
    do[...] = nt(da, wo[...]).astype(bf16)
    acc[...] += nn(o_t[...], da)

    @pl.when(at == pl.num_programs(0) - 1)
    def _():
        half = acc.shape[0] // 2
        mine = pl.multiple_of(info[0] * half, half)
        g_keep[...] = acc[pl.ds(mine, half), :].astype(bf16)
        g_send[...] = acc[pl.ds(half - mine, half), :].astype(bf16)


def middle(info, x2, m, dh, dy, o_t, weight, gain):
    seq, width = x2.shape
    rows = pl.BlockSpec((R, width), lambda i: (i, 0))
    half = whole((width // 2, width))
    return pl.pallas_call(
        middle_kernel,
        grid=(seq // R,),
        in_specs=[
            SMEM,
            rows,
            rows,
            rows,
            rows,
            pl.BlockSpec((width, R), lambda i: (0, i)),
            whole((width, width)),
            whole((1, width)),
        ],
        out_specs=[rows, rows, rows, half, half, whole((8, width))],
        out_shape=[shape((seq, width), bf16), shape((seq, width), f32), shape((seq, width), bf16)]
        + [shape((width // 2, width), bf16)] * 2
        + [shape((8, width), f32)],
        scratch_shapes=[pltpu.VMEM((width, width), f32)],
        compiler_params=params(40),
        cost_estimate=pl.CostEstimate(
            flops=4 * seq * width * width, bytes_accessed=26 * seq * width, transcendentals=0
        ),
        name="middle",
    )(info, x2, m, dh, dy, o_t, weight, gain)


def finish_kernel(
    info, x, dx2, dq, dko, dvo, dkc, dvc, rk, rv, cosine, minus, plus, h1t, wqkv, gain,
    dx, g_send, g_keep, sums, acc,
):
    at = pl.program_id(0)

    @pl.when(at == 0)
    def _():
        sums[...] = jnp.zeros_like(sums)
        acc[...] = jnp.zeros_like(acc)

    tables = (cosine[...], minus[...], plus[...], -1.0)
    clean = (1 - info[0]).astype(f32)
    total = lambda own, local, other: own[...] + clean * (local[...].astype(f32) + other[...].astype(f32))
    grads = jnp.concatenate(
        [
            rotated(dq[...], *tables).astype(bf16),
            rotated(total(dko, dkc, rk), *tables).astype(bf16),
            total(dvo, dvc, rv).astype(bf16),
        ],
        axis=1,
    )
    acc[...] += nn(h1t[...], grads)
    grad, gain_terms = norm_back(x[...].astype(f32), gain[...], nt(grads, wqkv[...]))
    sums[0:1, :] += row_sum(gain_terms)
    dx[...] = (dx2[...] + grad).astype(bf16)

    @pl.when(at == pl.num_programs(0) - 1)
    def _():
        half = acc.shape[0] // 2
        mine = pl.multiple_of(info[0] * half, half)
        g_keep[...] = acc[pl.ds(mine, half), :].astype(bf16)
        g_send[...] = acc[pl.ds(half - mine, half), :].astype(bf16)


def finish(info, x, dx2, dq, dko, dvo, dkc, dvc, rk, rv, tables, h1t, weight, gain):
    seq, width = x.shape
    wide = weight.shape[1]
    rows = pl.BlockSpec((R, width), lambda i: (i, 0))
    table = pl.BlockSpec((R, PW), lambda i: (i, 0))
    half = whole((width // 2, wide))
    return pl.pallas_call(
        finish_kernel,
        grid=(seq // R,),
        in_specs=[SMEM]
        + [rows] * 9
        + [table] * 3
        + [pl.BlockSpec((width, R), lambda i: (0, i)), whole((width, wide)), whole((1, width))],
        out_specs=[rows, half, half, whole((8, width))],
        out_shape=[shape((seq, width), bf16)]
        + [shape((width // 2, wide), bf16)] * 2
        + [shape((8, width), f32)],
        scratch_shapes=[pltpu.VMEM((width, wide), f32)],
        compiler_params=params(56),
        cost_estimate=pl.CostEstimate(
            flops=4 * seq * width * wide, bytes_accessed=40 * seq * width, transcendentals=0
        ),
        name="finish",
    )(info, x, dx2, dq, dko, dvo, dkc, dvc, rk, rv, *tables, h1t, weight, gain)


def bit_orders(count):
    bits = [1 << i for i in range(count.bit_length() - 1)]
    if len(bits) == 4:
        x, y, z, far = bits
        return [(x, y, z, far), (y, x, z, far), (z, x, far, y)]
    return [tuple(bits[g:] + bits[:g]) for g in range(GROUPS)]


def exchange(value, axis, bit):
    size = lax.axis_size(axis)
    return lax.ppermute(value, axis, [(i, i ^ bit) for i in range(size)])


def distance(order, place):
    out = 0
    for i, bit in enumerate(order):
        out = out + ((place >> (len(order) - 1 - i)) & 1) * bit
    return out


def start_kernel(arrays, me, *refs):
    ins = refs[: 2 * 2 * arrays * GROUPS]
    outs = refs[2 * 2 * arrays * GROUPS :]
    for g in range(GROUPS):
        for side in range(2):
            row = 0
            for a in range(arrays):
                base = ((g * 2 + side) * arrays + a) * 2
                kept, got = ins[base], ins[base + 1]
                size = kept.shape[1]
                total = kept[0].astype(f32) + got[0].astype(f32)
                outs[g * 2 + side][0, row : row + size, :] = total.astype(bf16)
                row += size


def start_sum(me, kept, got, views, orders):
    count = 1 << len(orders[0])
    half = count // 2
    specs, args, rows = [], [], 0
    for g, order in enumerate(orders):
        for side in range(2):
            for array, other, (block, place) in zip(kept, got, views, strict=True):
                index = lambda r, me, order=order, side=side, g=g, place=place: place(
                    me[0] ^ distance(order, r + side * half), g
                )
                specs += [pl.BlockSpec(block, index)] * 2
                args += [array, other]
    rows = sum(block[1] for block, _ in views)
    width = views[0][0][2]
    out = pl.BlockSpec((1, rows, width), lambda r, me: (r, 0, 0))
    outs = pl.pallas_call(
        functools.partial(start_kernel, len(kept)),
        grid_spec=pltpu.PrefetchScalarGridSpec(
            num_scalar_prefetch=1, grid=(half,), in_specs=specs, out_specs=[out] * (2 * GROUPS)
        ),
        out_shape=[shape((half, rows, width), bf16)] * (2 * GROUPS),
        cost_estimate=pl.CostEstimate(
            flops=0, bytes_accessed=6 * GROUPS * count * rows * width, transcendentals=0
        ),
        name="start_sum",
    )(me, *args)
    return outs[0::2], outs[1::2]


def step_kernel(*refs):
    for g in range(GROUPS):
        low, high, got_low, got_high = refs[4 * g : 4 * g + 4]
        keep, send = refs[4 * GROUPS + 2 * g : 4 * GROUPS + 2 * g + 2]
        keep[...] = (low[...].astype(f32) + got_low[...].astype(f32)).astype(bf16)
        send[...] = (high[...].astype(f32) + got_high[...].astype(f32)).astype(bf16)


def step_sum(kept, got):
    count, rows, width = kept[0].shape
    half = count // 2
    steps = min(half, 2)
    block = (half // steps, rows, width)
    low = pl.BlockSpec(block, lambda r: (r, 0, 0))
    high = pl.BlockSpec(block, lambda r: (r + steps, 0, 0))
    args = []
    for a, b in zip(kept, got, strict=True):
        args += [a, a, b, b]
    outs = pl.pallas_call(
        step_kernel,
        grid=(steps,),
        in_specs=[low, high, low, high] * GROUPS,
        out_specs=[low, low] * GROUPS,
        out_shape=[shape((half, rows, width), bf16)] * (2 * GROUPS),
        cost_estimate=pl.CostEstimate(
            flops=0, bytes_accessed=6 * GROUPS * count * rows * width, transcendentals=0
        ),
        name="step_sum",
    )(*args)
    return outs[0::2], outs[1::2]


def sum_parts(me, kept, got, views):
    orders = bit_orders(lax.axis_size("batch"))
    keep, send = start_sum(me, kept, got, views, orders)
    for i in range(len(orders[0])):
        got = [exchange(s, "batch", order[i]) for s, order in zip(send, orders, strict=True)]
        if i < len(orders[0]) - 1:
            keep, send = step_sum(keep, got)
    return [a[0].astype(f32) + b[0].astype(f32) for a, b in zip(keep, got, strict=True)]


def sum_all(value):
    value = value + exchange(value, "stream", 1)
    for order in bit_orders(lax.axis_size("batch"))[0]:
        value = value + exchange(value, "batch", order)
    return value


def on_device(
    inputs, lengths, cotangent, qkv_weight, out_weight, up_weight, down_weight, attn_gain, mlp_gain
):
    seq, width = inputs.shape[2:]
    x = inputs[0, 0]
    dy = cotangent[0, 0]
    count = lax.axis_size("batch")
    stream = lax.axis_index("stream").astype(jnp.int32)
    me = lax.axis_index("batch").astype(jnp.int32).reshape(1)
    info = jnp.stack([stream, lengths[0]])
    gain1, gain2 = attn_gain.reshape(1, width), mlp_gain.reshape(1, width)
    tables = [jnp.asarray(t) for t in rotary_tables(seq)]

    received = lax.ppermute(x, "stream", [(0, 1)])
    q, ko, vo, h1t, sums_x = project(info, x, gain1, qkv_weight, tables)
    kc, vc = clean_kv(info, x, received, gain1, qkv_weight, tables)
    o, o_t, lse = attend(info, q, ko, vo, kc, vc)
    x2, h2, sums_a = join(info, x, o, out_weight, gain2)

    part = stream.reshape(1)
    none = jnp.zeros((8, 128), f32)
    m, dh, up_send, down_send = feed(True, 1 - part, h2, dy, up_weight, down_weight, none, none)
    up_got, down_got = (exchange(a, "stream", 1) for a in (up_send, down_send))
    m, dh, up_keep, down_keep = feed(False, part, h2, dy, up_weight, down_weight, m, dh)
    outputs, dx2, do, out_send, out_keep, sums_m = middle(info, x2, m, dh, dy, o_t, out_weight, gain2)
    out_got = exchange(out_send, "stream", 1)

    def by_rows(array):
        return array.reshape(count * GROUPS, array.shape[0] // (count * GROUPS), width)

    def rows_view(array):
        return ((1, array.shape[0] // (count * GROUPS), width), lambda part, g: (part * GROUPS + g, 0, 0))

    kept = [down_keep, up_keep, out_keep]
    early = sum_parts(
        me,
        [by_rows(a) for a in kept],
        [by_rows(a) for a in (down_got, up_got, out_got)],
        [rows_view(a) for a in kept],
    )

    dq, dko, dvo, dkc, dvc = attend_back(info, q, ko, vo, kc, vc, o, do, lse)
    rk, rv = (lax.ppermute(a, "stream", [(1, 0)]) for a in (dkc, dvc))
    dx, qkv_send, qkv_keep, sums_h = finish(
        info, x, dx2, dq, dko, dvo, dkc, dvc, rk, rv, tables, h1t, qkv_weight, gain1
    )
    qkv_got = exchange(qkv_send, "stream", 1)
    tall = width // (2 * count)
    split = lambda a: a.reshape(count, tall, 3 * width)
    late = sum_parts(
        me, [split(qkv_keep)], [split(qkv_got)], [((1, tall, width), lambda part, g: (part, 0, g))]
    )
    small = jnp.concatenate(
        [
            sums_x[:1],
            sums_a[:1],
            sums_m[:2],
            sums_h[:1],
            jnp.full((1, width), lengths[0].astype(f32)),
            jnp.zeros((2, width), f32),
        ]
    )
    small = sum_all(small)

    tall = down_keep.shape[0] // (count * GROUPS)
    down_grad = jnp.concatenate([e[:tall] for e in early])
    up_grad = jnp.concatenate([e[tall : 2 * tall] for e in early]).T
    out_grad = jnp.concatenate([e[2 * tall :] for e in early])
    qkv_grad = jnp.concatenate(late, axis=1)
    squares = jnp.sum(small[jnp.array([0, 1, 2])], axis=1)
    rms = jnp.sqrt(squares / (small[5, 0] * width))
    return (
        outputs[None, None],
        dx[None, None],
        qkv_grad,
        out_grad,
        up_grad,
        down_grad,
        small[4],
        small[3],
        rms,
    )


def solution(mesh):
    rows = P("stream", "batch", None, None)
    both = ("stream", "batch")
    return jax.shard_map(
        on_device,
        mesh=mesh,
        in_specs=(rows, P("batch"), rows, P(), P(), P(), P(), P(), P()),
        out_specs=(rows, rows, P(both, None), P(both, None), P(None, both), P(both, None), P(), P(), P()),
        check_vma=False,
    )
```

time: 898 us -> 307 us (0.34)
  matrix products: 358 us -> 0 us
  waiting for transfers between devices: 320 us -> 50 us
  Pallas kernels: 0 us -> 182 us
  other arithmetic: 106 us -> 4.85 us
  blocking collectives: 44.9 us -> 0 us
  starting transfers between devices: 9.23 us -> 44.4 us
  local copies, waits for them, and re-layouts: 37.9 us -> 21.5 us
  between operations: 15.9 us -> 2.58 us
    reduce_scatter x4 -> x0, waiting for transfers between devices: 320 us -> none  [the longest x1 142 us: on_device(): lax.psum_scatter(down_grad, ('stream', 'batch'), scatter_dimension=0, til...]
    dot_general x22 -> x0, matrix products: 310 us -> none  [the longest x2 64.3 us: backward_row(): jnp.einsum('qhd,khd->hqk', g_part, v_row, preferred_element_type=jnp.floa...]
    pallas_call x0 -> x17, Pallas kernels: none -> 182 us  [the longest x2 51.2 us: feed(): pl.pallas_call(functools.partial(feed_kernel, first), grid_spec=pltpu.Pre...]
    convert_element_type x5 -> x0, other arithmetic: 83.4 us -> none  [the longest x2 81.2 us: backward_row(): grad_scores = grad_scores.astype(jnp.bfloat16)]
    ppermute x4 -> x36, waiting for transfers between devices: 0.01 us -> 50 us  [the longest x33 42 us: exchange(): return lax.ppermute(value, axis, [(i, i ^ bit) for i in range(size)])]
    sub x2 -> x0, matrix products: 47.9 us -> none  [forward_row(): expo = jnp.exp(scores - top)]
    psum x1 -> x0, blocking collectives: 44.9 us -> none  [on_device(): lax.psum((attn_gain_grad, mlp_gain_grad), ('stream', 'batch'))]
    ppermute x4 -> x36, starting transfers between devices: 9.07 us -> 44.4 us  [the longest x33 39.4 us: exchange(): return lax.ppermute(value, axis, [(i, i ^ bit) for i in range(size)])]
  transfers between devices with their start and end apart: 8 -> 36, of which waited for: 3 -> 13; matrix products, arithmetic and copies ran while one was open for 24% -> 2% of each run, Pallas kernels for 0% -> 17%
where the time goes in v1:
time: 307 us; the launch traced here: 305 us
  Pallas kernels  182 us (59%)
  waiting for transfers between devices  50 us (16%)
  starting transfers between devices  44.4 us (14%)
  local copies, waits for them, and re-layouts  21.5 us (7%)
  other arithmetic  4.85 us (2%)
    pallas_call x2, Pallas kernels, feed(): pl.pallas_call(functools.partial(feed_kernel, first), grid_spec=pltpu.Pre...  51.2 us
    ppermute x33, waiting for transfers between devices, exchange(): return lax.ppermute(value, axis, [(i, i ^ bit) for i in range(size)])  42 us
    ppermute x33, starting transfers between devices, exchange(): return lax.ppermute(value, axis, [(i, i ^ bit) for i in range(size)])  39.4 us
    pallas_call x1, Pallas kernels, attend_back(): pl.pallas_call(attend_back_kernel, grid=(pairs,), in_specs=[SMEM] + [cols...  37.2 us
    pallas_call x1, Pallas kernels, attend(): pl.pallas_call(attend_kernel, grid=(pairs,), in_specs=[SMEM] + [cols] * 5...  23 us
    pallas_call x1, Pallas kernels, finish(): pl.pallas_call(finish_kernel, grid=(seq // R,), in_specs=[SMEM] + [rows]...  17.5 us
    unnamed x108, local copies, waits for them, and re-layouts  16.9 us
    pallas_call x2, Pallas kernels, start_sum(): pl.pallas_call(functools.partial(start_kernel, len(kept)), grid_spec=pltp...  15.1 us
  transfers between devices with their start and end apart: 36, of which 13 were waited for; matrix products, arithmetic and copies ran while one was open for 2% of the time, Pallas kernels for 17%

profile of v1, /device:TPU:0, one launch (start us, length us, event | category | flops | bytes accessed | tf_op | source)
XLA Modules:
  0.0 304.9 jit_solution(9924637093154430452)
XLA Ops:
  0.6 2.5 collective-permute-start
  5.2 2.0 copy-done
  11.8 6.6 %project.1 = (bf16[1024,768]{1,0:T(8,128)(2,1)S(1)}, bf16[1024,768]{1,0:T(8,128)(2,1)S(1)}, bf16[1024,768]{1,0:T(8,128)(2,1)S(1)}, bf16[768,1024]{1,0:T(8,128)(2,1)S(1)}, f32[8,768]{1,0:T(8,128)S(1)}) custom-call(s32[2]{0:T(128)S(1)} %pad_add_fusion.info, bf16[1024,768]{1,0:T(8,128)(2,1)S(1)} %bitcast.50, f32[1,768]{1,0:T(1,128)S(1)} %reshape.82.gain, ...), custom_call_target="tpu_custom_call" | custom-call | flops 3623878656 | bytes 9437184 | tf_op jit(solution)/shard_map/project/pallas_call | solution.py:115
  18.5 4.4 %clean_kv.1 = (bf16[1024,768]{1,0:T(8,128)(2,1)S(1)}, bf16[1024,768]{1,0:T(8,128)(2,1)S(1)}) custom-call(s32[2]{0:T(128)S(1)} %pad_add_fusion.info, bf16[1024,768]{1,0:T(8,128)(2,1)S(1)} %bitcast.51, bf16[1024,768]{1,0:T(8,128)(2,1)S(1)} %collective-permute-done.received, f32[1,768]{1,0:T(1,128)S(1)} %reshape.82.gain, bf16[768,2304]{1,0:T(8,128)(2,1)S(1)} %copy-done, ...), custom_call_target="tpu_custom_call" | custom-call | flops 2415919104 | bytes 7864320 | tf_op jit(solution)/shard_map/clean_kv/pallas_call | solution.py:141
  22.9 23.0 %attend.1 = (bf16[1024,768]{1,0:T(8,128)(2,1)S(1)}, bf16[768,1024]{1,0:T(8,128)(2,1)S(1)}, f32[6,8,256]{2,1,0:T(8,128)S(1)}) custom-call(s32[2]{0:T(128)S(1)} %pad_add_fusion.info, bf16[1024,768]{1,0:T(8,128)(2,1)S(1)} %get-tuple-element.93.q, bf16[1024,768]{1,0:T(8,128)(2,1)S(1)} %get-tuple-element.94.ko, bf16[1024,768]{1,0:T(8,128)(2,1)S(1)} %get-tuple-element.95.vo, ...), custom_call_target="tpu_custom_call" | custom-call | flops 3221225472 | bytes 11010048 | tf_op jit(solution)/shard_map/attend/pallas_call | solution.py:232
  46.0 3.2 %join.1 = (f32[1024,768]{1,0:T(8,128)S(1)}, bf16[1024,768]{1,0:T(8,128)(2,1)S(1)}, f32[8,768]{1,0:T(8,128)S(1)}) custom-call(s32[2]{0:T(128)S(1)} %pad_add_fusion.info, bf16[1024,768]{1,0:T(8,128)(2,1)S(1)} %bitcast.52, bf16[1024,768]{1,0:T(8,128)(2,1)S(1)} %get-tuple-element.98.o, bf16[768,768]{1,0:T(8,128)(2,1)S(1)} %copy-done.12, f32[1,768]{1,0:T(1,128)S(1)} %reshape.83.gain), custom_call_target="tpu_custom_call" | custom-call | flops 1207959552 | bytes 7864320 | tf_op jit(solution)/shard_map/join/pallas_call | solution.py:329
  50.9 24.4 %feed.2 = (f32[1024,768]{1,0:T(8,128)}, f32[1024,768]{1,0:T(8,128)}, bf16[1536,768]{1,0:T(8,128)(2,1)}, bf16[1536,768]{1,0:T(8,128)(2,1)}) custom-call(s32[1]{0:T(128)S(6)} %sub.3.at, bf16[1024,768]{1,0:T(8,128)(2,1)} %copy-done.27, bf16[1024,768]{1,0:T(8,128)(2,1)} %bitcast.53, bf16[768,3072]{1,0:T(8,128)(2,1)} %w1.3, bf16[3072,768]{1,0:T(8,128)(2,1)} %w2.3, ...), custom_call_target="tpu_custom_call" | custom-call | flops 14495514624 | bytes 18874368 | tf_op jit(solution)/shard_map/feed/pallas_call | solution.py:383
  75.3 26.7 %feed.3 = (f32[1024,768]{1,0:T(8,128)}, f32[1024,768]{1,0:T(8,128)}, bf16[1536,768]{1,0:T(8,128)(2,1)}, bf16[1536,768]{1,0:T(8,128)(2,1)}) custom-call(s32[1]{0:T(128)} %bitcast.at, bf16[1024,768]{1,0:T(8,128)(2,1)} %copy-done.27, bf16[1024,768]{1,0:T(8,128)(2,1)} %bitcast.54, bf16[768,3072]{1,0:T(8,128)(2,1)} %w1.3, bf16[3072,768]{1,0:T(8,128)(2,1)} %w2.3, ...), custom_call_target="tpu_custom_call" | custom-call | flops 14495514624 | bytes 18874368 | tf_op jit(solution)/shard_map/feed/pallas_call | solution.py:383
  102.1 8.6 %middle.1 = (bf16[1024,768]{1,0:T(8,128)(2,1)}, f32[1024,768]{1,0:T(8,128)S(1)}, bf16[1024,768]{1,0:T(8,128)(2,1)S(1)}, bf16[384,768]{1,0:T(8,128)(2,1)S(1)}, bf...) custom-call(s32[2]{0:T(128)S(1)} %pad_add_fusion.info, f32[1024,768]{1,0:T(8,128)S(1)} %get-tuple-element.99.x2, ...), custom_call_target="tpu_custom_call" | custom-call | flops 2415919104 | bytes 20447232 | tf_op jit(solution)/shard_map/middle/pallas_call | solution.py:440
  113.3 37.2 %attend_back.1 = (f32[1024,768]{1,0:T(8,128)}, f32[1024,768]{1,0:T(8,128)}, f32[1024,768]{1,0:T(8,128)}, bf16[1024,768]{1,0:T(8,128)(2,1)S(1)}, bf16[1024,768]{1,0:T(8,128)(2,1)S(1)}) custom-call(s32[2]{0:T(128)S(1)} %pad_add_fusion.info, bf16[1024,768]{1,0:T(8,128)(2,1)S(1)} %copy-done.16, bf16[1024,768]{1,0:T(8,128)(2,1)S(1)} %copy-done.18, ...), custom_call_target="tpu_custom_call" | custom-call | flops 6442450944 | bytes 23592960 | tf_op jit(solution)/shard_map/attend_back/pallas_call | solution.py:296
  155.8 6.7 %collective-permute-done.2.rv = bf16[1024,768]{1,0:T(8,128)(2,1)S(1)} collective-permute-done((bf16[1024,768]{1,0:T(8,128)(2,1)S(1)}, bf16[1024,768]{1,0:T(8,128)(2,1)S(1)}, u32[]{:S(2)}, u32[]{:S(2)}) %collective-permute-start.2) | collective-permute-done | bytes 1572896 | tf_op jit(solution)/shard_map/ppermute | solution.py:682
  163.7 17.5 %finish.1 = (bf16[1024,768]{1,0:T(8,128)(2,1)}, bf16[384,2304]{1,0:T(8,128)(2,1)}, bf16[384,2304]{1,0:T(8,128)(2,1)}, f32[8,768]{1,0:T(8,128)}) custom-call(s32[2]{0:T(128)} %copy-done.14, bf16[1024,768]{1,0:T(8,128)(2,1)} %bitcast.49, f32[1024,768]{1,0:T(8,128)} %copy-done.7, f32[1024,768]{1,0:T(8,128)} %get-tuple-element.110.dq, ...), custom_call_target="tpu_custom_call" | custom-call | flops 7247757312 | bytes 31457280 | tf_op jit(solution)/shard_map/finish/pallas_call | solution.py:507
  181.8 4.1 %collective-permute-done.18 = bf16[384,768]{1,0:T(8,128)(2,1)} collective-permute-done((bf16[384,768]{1,0:T(8,128)(2,1)S(1)}, bf16[384,768]{1,0:T(8,128)(2,1)}, u32[]{:S(2)}, u32[]{:S(2)}) %collective-permute-start.18) | collective-permute-done | bytes 589856 | tf_op jit(solution)/shard_map/ppermute | solution.py:537
  187.4 9.2 %start_sum.3 = (bf16[8,72,768]{2,1,0:T(8,128)(2,1)}, bf16[8,72,768]{2,1,0:T(8,128)(2,1)}, bf16[8,72,768]{2,1,0:T(8,128)(2,1)}, bf16[8,72,768]{2,1,0:T(8,128)(2,1...) custom-call(s32[1]{0:T(128)} %bitcast.5.me, bf16[48,32,768]{2,1,0:T(8,128)(2,1)} %bitcast.62, ...), custom_call_target="tpu_custom_call" | custom-call | bytes 15925248 | tf_op jit(solution)/shard_map/start_sum/pallas_call | solution.py:577
  196.6 2.3 collective-permute-start.19
  202.0 5.9 %start_sum.2 = (bf16[8,24,768]{2,1,0:T(8,128)(2,1)}, bf16[8,24,768]{2,1,0:T(8,128)(2,1)}, bf16[8,24,768]{2,1,0:T(8,128)(2,1)}, bf16[8,24,768]{2,1,0:T(8,128)(2,1...) custom-call(s32[1]{0:T(128)} %bitcast.5.me, bf16[16,24,2304]{2,1,0:T(8,128)(2,1)} %bitcast.74, ...), custom_call_target="tpu_custom_call" | custom-call | bytes 5308416 | tf_op jit(solution)/shard_map/start_sum/pallas_call | solution.py:577
  212.1 13.9 %collective-permute-done.32 = f32[8,768]{1,0:T(8,128)S(1)} collective-permute-done((f32[8,768]{1,0:T(8,128)S(1)}, f32[8,768]{1,0:T(8,128)S(1)}, u32[]{:S(2)}, u32[]{:S(2)}) %collective-permute-start.32) | collective-permute-done | bytes 24608 | tf_op jit(solution)/shard_map/ppermute | solution.py:537
  226.0 1.8 collective-permute-start.33
  227.7 2.1 collective-permute-done.33
  233.2 4.3 %collective-permute-done.5.refs_6_.refs_7_ = bf16[8,24,768]{2,1,0:T(8,128)(2,1)S(1)} collective-permute-done((bf16[8,24,768]{2,1,0:T(8,128)(2,1)}, bf16[8,24,768]{2,1,0:T(8,128)(2,1)S(1)}, u32[]{:S(2)}, u32[]{:S(2)}) %collective-permute-start.5) | collective-permute-done | bytes 294944 | tf_op jit(solution)/shard_map/ppermute | solution.py:537
  239.0 2.3 step_sum.6
  245.0 2.7 collective-permute-start.35
  248.6 4.0 %step_sum.9 = (bf16[4,72,768]{2,1,0:T(8,128)(2,1)}, bf16[4,72,768]{2,1,0:T(8,128)(2,1)}, bf16[4,72,768]{2,1,0:T(8,128)(2,1)}, bf16[4,72,768]{2,1,0:T(8,128)(2,1)...) custom-call(bf16[8,72,768]{2,1,0:T(8,128)(2,1)} %get-tuple-element.149.refs_0_.refs_1_, ...), custom_call_target="tpu_custom_call" | custom-call | bytes 7962624 | tf_op jit(solution)/shard_map/step_sum/pallas_call | solution.py:609
  255.8 1.9 step_sum.7
  263.6 2.2 collective-permute-done.11.refs_6_.refs_7_
  265.8 1.9 collective-permute-done.12.refs_10_.refs_11_
  273.0 2.8 step_sum.10
  275.8 2.5 collective-permute-start.25
  282.9 7.1 %collective-permute-done.14 = bf16[1,24,768]{2,1,0:T(8,128)(2,1)S(1)} collective-permute-done((bf16[1,24,768]{2,1,0:T(8,128)(2,1)S(1)}, bf16[1,24,768]{2,1,0:T(8,128)(2,1)S(1)}, u32[]{:S(2)}, u32[]{:S(2)}) %collective-permute-start.14) | collective-permute-done | bytes 36896 | tf_op jit(solution)/shard_map/ppermute | solution.py:537
  290.9 2.3 step_sum.11
  293.2 2.6 collective-permute-start.28
  296.9 4.0 %collective-permute-done.28 = bf16[1,72,768]{2,1,0:T(8,128)(2,1)S(1)} collective-permute-done((bf16[1,72,768]{2,1,0:T(8,128)(2,1)}, bf16[1,72,768]{2,1,0:T(8,128)(2,1)S(1)}, u32[]{:S(2)}, u32[]{:S(2)}) %collective-permute-start.28) | collective-permute-done | bytes 110624 | tf_op jit(solution)/shard_map/ppermute | solution.py:537
  (203 shorter events, 59.7 us)
Async XLA Ops:
  0.6 17.8 %collective-permute-start = (bf16[1024,768]{1,0:T(8,128)(2,1)}, bf16[1024,768]{1,0:T(8,128)(2,1)S(1)}, u32[]{:S(2)}, u32[]{:S(2)}) collective-permute-start(bf16[1024,768]{1,0:T(8,128)(2,1)} %bitcast.48), channel_id=1, source_target_pairs={{0,16},{1,17},{2,18},{3,19},{4,20},{5,21},{6,22},{7,23},{8,24},{9,... | collective-permute-start | bytes 4718600 | tf_op jit(solution)/shard_map/ppermute | solution.py:653
  150.5 5.3 %collective-permute-start.1 = (bf16[1024,768]{1,0:T(8,128)(2,1)S(1)}, bf16[1024,768]{1,0:T(8,128)(2,1)S(1)}, u32[]{:S(2)}, u32[]{:S(2)}) collective-permute-start(bf16[1024,768]{1,0:T(8,128)(2,1)S(1)} %get-tuple-element.113.dkc), channel_id=1, source_target_pairs={{16,0},{17,1},{18,2},{19,3},{20,4},{21,5},{22,6},{23,7},{24,8},{25... | collective-permute-start | bytes 4718600 | tf_op jit(solution)/shard_map/ppermute | solution.py:682
  151.8 10.8 %collective-permute-start.2 = (bf16[1024,768]{1,0:T(8,128)(2,1)S(1)}, bf16[1024,768]{1,0:T(8,128)(2,1)S(1)}, u32[]{:S(2)}, u32[]{:S(2)}) collective-permute-start(bf16[1024,768]{1,0:T(8,128)(2,1)S(1)} %get-tuple-element.114.dvc), channel_id=1, source_target_pairs={{16,0},{17,1},{18,2},{19,3},{20,4},{21,5},{22,6},{23,7},{24,8},{25... | collective-permute-start | bytes 4718600 | tf_op jit(solution)/shard_map/ppermute | solution.py:682
  153.1 32.8 %collective-permute-start.16 = (bf16[1536,768]{1,0:T(8,128)(2,1)}, bf16[1536,768]{1,0:T(8,128)(2,1)S(1)}, u32[]{:S(2)}, u32[]{:S(2)}) collective-permute-start(bf16[1536,768]{1,0:T(8,128)(2,1)} %get-tuple-element.144), channel_id=1, source_target_pairs={{0,16},{16,0},{1,17},{17,1},{2,18},{18,2},{3,19},{19,3},{4,20},{20... | collective-permute-start | bytes 7077896 | tf_op jit(solution)/shard_map/ppermute | solution.py:537
  154.5 31.4 %collective-permute-start.17 = (bf16[1536,768]{1,0:T(8,128)(2,1)}, bf16[1536,768]{1,0:T(8,128)(2,1)}, u32[]{:S(2)}, u32[]{:S(2)}) collective-permute-start(bf16[1536,768]{1,0:T(8,128)(2,1)} %get-tuple-element.146), channel_id=1, source_target_pairs={{0,16},{16,0},{1,17},{17,1},{2,18},{18,2},{3,19},{19,3},{4,20},{20... | collective-permute-start | bytes 7077896 | tf_op jit(solution)/shard_map/ppermute | solution.py:537
  181.2 20.8 %collective-permute-start.3 = (bf16[384,2304]{1,0:T(8,128)(2,1)}, bf16[384,2304]{1,0:T(8,128)(2,1)}, u32[]{:S(2)}, u32[]{:S(2)}) collective-permute-start(bf16[384,2304]{1,0:T(8,128)(2,1)} %get-tuple-element.118), channel_id=1, source_target_pairs={{0,16},{16,0},{1,17},{17,1},{2,18},{18,2},{3,19},{19,3},{4,20},{20... | collective-permute-start | bytes 5308424 | tf_op jit(solution)/shard_map/ppermute | solution.py:537
  196.6 47.8 %collective-permute-start.19 = (bf16[8,72,768]{2,1,0:T(8,128)(2,1)}, bf16[8,72,768]{2,1,0:T(8,128)(2,1)S(1)}, u32[]{:S(2)}, u32[]{:S(2)}) collective-permute-start(bf16[8,72,768]{2,1,0:T(8,128)(2,1)} %get-tuple-element.150), channel_id=1, source_target_pairs={{0,1},{1,0},{2,3},{3,2},{4,5},{5,4},{6,7},{7,6},{8,9},{9,8},{10,11... | collective-permute-start | bytes 2654216 | tf_op jit(solution)/shard_map/ppermute | solution.py:537
  198.9 46.0 %collective-permute-start.20 = (bf16[8,72,768]{2,1,0:T(8,128)(2,1)}, bf16[8,72,768]{2,1,0:T(8,128)(2,1)S(1)}, u32[]{:S(2)}, u32[]{:S(2)}) collective-permute-start(bf16[8,72,768]{2,1,0:T(8,128)(2,1)} %get-tuple-element.152), channel_id=1, source_target_pairs={{0,2},{1,3},{2,0},{3,1},{4,6},{5,7},{6,4},{7,5},{8,10},{9,11},{10,... | collective-permute-start | bytes 2654216 | tf_op jit(solution)/shard_map/ppermute | solution.py:537
  200.4 47.2 %collective-permute-start.21 = (bf16[8,72,768]{2,1,0:T(8,128)(2,1)}, bf16[8,72,768]{2,1,0:T(8,128)(2,1)S(1)}, u32[]{:S(2)}, u32[]{:S(2)}) collective-permute-start(bf16[8,72,768]{2,1,0:T(8,128)(2,1)} %get-tuple-element.154), channel_id=1, source_target_pairs={{0,4},{1,5},{2,6},{3,7},{4,0},{5,1},{6,2},{7,3},{8,12},{9,13},{10,... | collective-permute-start | bytes 2654216 | tf_op jit(solution)/shard_map/ppermute | solution.py:537
  207.9 23.6 %collective-permute-start.4 = (bf16[8,24,768]{2,1,0:T(8,128)(2,1)}, bf16[8,24,768]{2,1,0:T(8,128)(2,1)S(1)}, u32[]{:S(2)}, u32[]{:S(2)}) collective-permute-start(bf16[8,24,768]{2,1,0:T(8,128)(2,1)} %get-tuple-element.120), channel_id=1, source_target_pairs={{0,1},{1,0},{2,3},{3,2},{4,5},{5,4},{6,7},{7,6},{8,9},{9,8},{10,11... | collective-permute-start | bytes 884744 | tf_op jit(solution)/shard_map/ppermute | solution.py:537
  210.6 15.4 %collective-permute-start.32 = (f32[8,768]{1,0:T(8,128)S(1)}, f32[8,768]{1,0:T(8,128)S(1)}, u32[]{:S(2)}, u32[]{:S(2)}) collective-permute-start(f32[8,768]{1,0:T(8,128)S(1)} %add.57), channel_id=1, source_target_pairs={{0,1},{1,0},{2,3},{3,2},{4,5},{5,4},{6,7},{7,6},{8,9},{9,8},{10,11... | collective-permute-start | bytes 73736 | tf_op jit(solution)/shard_map/ppermute | solution.py:537
  229.8 7.7 %collective-permute-start.5 = (bf16[8,24,768]{2,1,0:T(8,128)(2,1)}, bf16[8,24,768]{2,1,0:T(8,128)(2,1)S(1)}, u32[]{:S(2)}, u32[]{:S(2)}) collective-permute-start(bf16[8,24,768]{2,1,0:T(8,128)(2,1)} %get-tuple-element.122), channel_id=1, source_target_pairs={{0,2},{1,3},{2,0},{3,1},{4,6},{5,7},{6,4},{7,5},{8,10},{9,11},{10,... | collective-permute-start | bytes 884744 | tf_op jit(solution)/shard_map/ppermute | solution.py:537
  231.6 7.4 %collective-permute-start.6 = (bf16[8,24,768]{2,1,0:T(8,128)(2,1)}, bf16[8,24,768]{2,1,0:T(8,128)(2,1)}, u32[]{:S(2)}, u32[]{:S(2)}) collective-permute-start(bf16[8,24,768]{2,1,0:T(8,128)(2,1)} %get-tuple-element.124), channel_id=1, source_target_pairs={{0,4},{1,5},{2,6},{3,7},{4,0},{5,1},{6,2},{7,3},{8,12},{9,13},{10,... | collective-permute-start | bytes 884744 | tf_op jit(solution)/shard_map/ppermute | solution.py:537
  237.5 5.5 %collective-permute-start.34 = (f32[8,768]{1,0:T(8,128)S(1)}, f32[8,768]{1,0:T(8,128)S(1)}, u32[]{:S(2)}, u32[]{:S(2)}) collective-permute-start(f32[8,768]{1,0:T(8,128)S(1)} %add.59), channel_id=1, source_target_pairs={{0,4},{1,5},{2,6},{3,7},{4,0},{5,1},{6,2},{7,3},{8,12},{9,13},{10,... | collective-permute-start | bytes 73736 | tf_op jit(solution)/shard_map/ppermute | solution.py:537
  241.3 11.8 %collective-permute-start.7 = (bf16[4,24,768]{2,1,0:T(8,128)(2,1)}, bf16[4,24,768]{2,1,0:T(8,128)(2,1)S(1)}, u32[]{:S(2)}, u32[]{:S(2)}) collective-permute-start(bf16[4,24,768]{2,1,0:T(8,128)(2,1)} %get-tuple-element.126), channel_id=1, source_target_pairs={{0,2},{1,3},{2,0},{3,1},{4,6},{5,7},{6,4},{7,5},{8,10},{9,11},{10,... | collective-permute-start | bytes 442376 | tf_op jit(solution)/shard_map/ppermute | solution.py:537
  242.9 11.7 %collective-permute-start.8 = (bf16[4,24,768]{2,1,0:T(8,128)(2,1)}, bf16[4,24,768]{2,1,0:T(8,128)(2,1)S(1)}, u32[]{:S(2)}, u32[]{:S(2)}) collective-permute-start(bf16[4,24,768]{2,1,0:T(8,128)(2,1)} %get-tuple-element.128), channel_id=1, source_target_pairs={{0,1},{1,0},{2,3},{3,2},{4,5},{5,4},{6,7},{7,6},{8,9},{9,8},{10,11... | collective-permute-start | bytes 442376 | tf_op jit(solution)/shard_map/ppermute | solution.py:537
  244.4 10.7 %collective-permute-start.9 = (bf16[4,24,768]{2,1,0:T(8,128)(2,1)}, bf16[4,24,768]{2,1,0:T(8,128)(2,1)S(1)}, u32[]{:S(2)}, u32[]{:S(2)}) collective-permute-start(bf16[4,24,768]{2,1,0:T(8,128)(2,1)} %get-tuple-element.130), channel_id=1, source_target_pairs={{0,1},{1,0},{2,3},{3,2},{4,5},{5,4},{6,7},{7,6},{8,9},{9,8},{10,11... | collective-permute-start | bytes 442376 | tf_op jit(solution)/shard_map/ppermute | solution.py:537
  245.0 14.4 %collective-permute-start.35 = (f32[8,768]{1,0:T(8,128)S(1)}, f32[8,768]{1,0:T(8,128)S(1)}, u32[]{:S(2)}, u32[]{:S(2)}) collective-permute-start(f32[8,768]{1,0:T(8,128)S(1)} %add.60), channel_id=1, source_target_pairs={{0,8},{1,9},{2,10},{3,11},{4,12},{5,13},{6,14},{7,15},{8,0},{9,1},... | collective-permute-start | bytes 73736 | tf_op jit(solution)/shard_map/ppermute | solution.py:537
  252.5 19.4 %collective-permute-start.22 = (bf16[4,72,768]{2,1,0:T(8,128)(2,1)}, bf16[4,72,768]{2,1,0:T(8,128)(2,1)S(1)}, u32[]{:S(2)}, u32[]{:S(2)}) collective-permute-start(bf16[4,72,768]{2,1,0:T(8,128)(2,1)} %get-tuple-element.156), channel_id=1, source_target_pairs={{0,2},{1,3},{2,0},{3,1},{4,6},{5,7},{6,4},{7,5},{8,10},{9,11},{10,... | collective-permute-start | bytes 1327112 | tf_op jit(solution)/shard_map/ppermute | solution.py:537
  253.1 18.8 %collective-permute-start.23 = (bf16[4,72,768]{2,1,0:T(8,128)(2,1)}, bf16[4,72,768]{2,1,0:T(8,128)(2,1)S(1)}, u32[]{:S(2)}, u32[]{:S(2)}) collective-permute-start(bf16[4,72,768]{2,1,0:T(8,128)(2,1)} %get-tuple-element.158), channel_id=1, source_target_pairs={{0,1},{1,0},{2,3},{3,2},{4,5},{5,4},{6,7},{7,6},{8,9},{9,8},{10,11... | collective-permute-start | bytes 1327112 | tf_op jit(solution)/shard_map/ppermute | solution.py:537
  254.6 17.4 %collective-permute-start.24 = (bf16[4,72,768]{2,1,0:T(8,128)(2,1)}, bf16[4,72,768]{2,1,0:T(8,128)(2,1)S(1)}, u32[]{:S(2)}, u32[]{:S(2)}) collective-permute-start(bf16[4,72,768]{2,1,0:T(8,128)(2,1)} %get-tuple-element.160), channel_id=1, source_target_pairs={{0,1},{1,0},{2,3},{3,2},{4,5},{5,4},{6,7},{7,6},{8,9},{9,8},{10,11... | collective-permute-start | bytes 1327112 | tf_op jit(solution)/shard_map/ppermute | solution.py:537
  261.2 4.6 %collective-permute-start.11 = (bf16[2,24,768]{2,1,0:T(8,128)(2,1)}, bf16[2,24,768]{2,1,0:T(8,128)(2,1)S(1)}, u32[]{:S(2)}, u32[]{:S(2)}) collective-permute-start(bf16[2,24,768]{2,1,0:T(8,128)(2,1)} %get-tuple-element.134), channel_id=1, source_target_pairs={{0,4},{1,5},{2,6},{3,7},{4,0},{5,1},{6,2},{7,3},{8,12},{9,13},{10,... | collective-permute-start | bytes 221192 | tf_op jit(solution)/shard_map/ppermute | solution.py:537
  262.3 5.5 %collective-permute-start.12 = (bf16[2,24,768]{2,1,0:T(8,128)(2,1)}, bf16[2,24,768]{2,1,0:T(8,128)(2,1)S(1)}, u32[]{:S(2)}, u32[]{:S(2)}) collective-permute-start(bf16[2,24,768]{2,1,0:T(8,128)(2,1)} %get-tuple-element.136), channel_id=1, source_target_pairs={{0,8},{1,9},{2,10},{3,11},{4,12},{5,13},{6,14},{7,15},{8,0},{9,1},... | collective-permute-start | bytes 221192 | tf_op jit(solution)/shard_map/ppermute | solution.py:537
  270.1 11.3 %collective-permute-start.13 = (bf16[1,24,768]{2,1,0:T(8,128)(2,1)}, bf16[1,24,768]{2,1,0:T(8,128)(2,1)S(1)}, u32[]{:S(2)}, u32[]{:S(2)}) collective-permute-start(bf16[1,24,768]{2,1,0:T(8,128)(2,1)} %get-tuple-element.138), channel_id=1, source_target_pairs={{0,8},{1,9},{2,10},{3,11},{4,12},{5,13},{6,14},{7,15},{8,0},{9,1},... | collective-permute-start | bytes 110600 | tf_op jit(solution)/shard_map/ppermute | solution.py:537
  275.8 14.3 %collective-permute-start.25 = (bf16[2,72,768]{2,1,0:T(8,128)(2,1)}, bf16[2,72,768]{2,1,0:T(8,128)(2,1)S(1)}, u32[]{:S(2)}, u32[]{:S(2)}) collective-permute-start(bf16[2,72,768]{2,1,0:T(8,128)(2,1)} %get-tuple-element.162), channel_id=1, source_target_pairs={{0,4},{1,5},{2,6},{3,7},{4,0},{5,1},{6,2},{7,3},{8,12},{9,13},{10,... | collective-permute-start | bytes 663560 | tf_op jit(solution)/shard_map/ppermute | solution.py:537
  278.3 11.8 %collective-permute-start.26 = (bf16[2,72,768]{2,1,0:T(8,128)(2,1)}, bf16[2,72,768]{2,1,0:T(8,128)(2,1)S(1)}, u32[]{:S(2)}, u32[]{:S(2)}) collective-permute-start(bf16[2,72,768]{2,1,0:T(8,128)(2,1)} %get-tuple-element.164), channel_id=1, source_target_pairs={{0,4},{1,5},{2,6},{3,7},{4,0},{5,1},{6,2},{7,3},{8,12},{9,13},{10,... | collective-permute-start | bytes 663560 | tf_op jit(solution)/shard_map/ppermute | solution.py:537
  278.4 11.7 %collective-permute-start.27 = (bf16[2,72,768]{2,1,0:T(8,128)(2,1)}, bf16[2,72,768]{2,1,0:T(8,128)(2,1)S(1)}, u32[]{:S(2)}, u32[]{:S(2)}) collective-permute-start(bf16[2,72,768]{2,1,0:T(8,128)(2,1)} %get-tuple-element.166), channel_id=1, source_target_pairs={{0,8},{1,9},{2,10},{3,11},{4,12},{5,13},{6,14},{7,15},{8,0},{9,1},... | collective-permute-start | bytes 663560 | tf_op jit(solution)/shard_map/ppermute | solution.py:537
  279.6 10.4 %collective-permute-start.14 = (bf16[1,24,768]{2,1,0:T(8,128)(2,1)S(1)}, bf16[1,24,768]{2,1,0:T(8,128)(2,1)S(1)}, u32[]{:S(2)}, u32[]{:S(2)}) collective-permute-start(bf16[1,24,768]{2,1,0:T(8,128)(2,1)S(1)} %copy-done.53), channel_id=1, source_target_pairs={{0,8},{1,9},{2,10},{3,11},{4,12},{5,13},{6,14},{7,15},{8,0},{9,1},... | collective-permute-start | bytes 110600 | tf_op jit(solution)/shard_map/ppermute | solution.py:537
  281.3 8.7 %collective-permute-start.15 = (bf16[1,24,768]{2,1,0:T(8,128)(2,1)S(1)}, bf16[1,24,768]{2,1,0:T(8,128)(2,1)S(1)}, u32[]{:S(2)}, u32[]{:S(2)}) collective-permute-start(bf16[1,24,768]{2,1,0:T(8,128)(2,1)S(1)} %copy-done.52), channel_id=1, source_target_pairs={{0,2},{1,3},{2,0},{3,1},{4,6},{5,7},{6,4},{7,5},{8,10},{9,11},{10,... | collective-permute-start | bytes 110600 | tf_op jit(solution)/shard_map/ppermute | solution.py:537
  293.2 7.6 %collective-permute-start.28 = (bf16[1,72,768]{2,1,0:T(8,128)(2,1)}, bf16[1,72,768]{2,1,0:T(8,128)(2,1)S(1)}, u32[]{:S(2)}, u32[]{:S(2)}) collective-permute-start(bf16[1,72,768]{2,1,0:T(8,128)(2,1)} %get-tuple-element.168), channel_id=1, source_target_pairs={{0,8},{1,9},{2,10},{3,11},{4,12},{5,13},{6,14},{7,15},{8,0},{9,1},... | collective-permute-start | bytes 331784 | tf_op jit(solution)/shard_map/ppermute | solution.py:537
  296.5 5.9 %collective-permute-start.29 = (bf16[1,72,768]{2,1,0:T(8,128)(2,1)}, bf16[1,72,768]{2,1,0:T(8,128)(2,1)S(1)}, u32[]{:S(2)}, u32[]{:S(2)}) collective-permute-start(bf16[1,72,768]{2,1,0:T(8,128)(2,1)} %get-tuple-element.170), channel_id=1, source_target_pairs={{0,8},{1,9},{2,10},{3,11},{4,12},{5,13},{6,14},{7,15},{8,0},{9,1},... | collective-permute-start | bytes 331784 | tf_op jit(solution)/shard_map/ppermute | solution.py:537
  296.9 6.4 %collective-permute-start.30 = (bf16[1,72,768]{2,1,0:T(8,128)(2,1)}, bf16[1,72,768]{2,1,0:T(8,128)(2,1)S(1)}, u32[]{:S(2)}, u32[]{:S(2)}) collective-permute-start(bf16[1,72,768]{2,1,0:T(8,128)(2,1)} %get-tuple-element.172), channel_id=1, source_target_pairs={{0,2},{1,3},{2,0},{3,1},{4,6},{5,7},{6,4},{7,5},{8,10},{9,11},{10,... | collective-permute-start | bytes 331784 | tf_op jit(solution)/shard_map/ppermute | solution.py:537
  (58 other events, 484.7 us)
